TPU v7x, 768 devices: a whole 4x8x12 slice. The times are simulated.
768 devices in a mesh: elem: 96 (over y, z), clus: 8 (over x, core).
Axes of the slice: x: 4, y: 8, z: 12, core: 2. Of those that a mesh axis runs over, the one named last changes fastest.
Arguments:
- nodal: float32 [512, 196608], P(None, ('elem', 'clus')), may hold values from -6 to 6
- metric: bfloat16 [3, 512, 196608], P(None, None, ('elem', 'clus')), may hold values from 0.25 to 2.5
- derivative: float32 [8, 8], replicated, may hold values from -2 to 2
- interp: float32 [2, 8, 8], replicated, may hold values from -2 to 2
- face_level: int32 [1179648], P(('elem', 'clus')), may hold values from 0 to 4
- face_target: int32 [1179648], P(('elem', 'clus')), may hold values from 0 to 895, as said below
- slot_mortar: int32 [294912], P(('elem', 'clus')), may hold values from 0 to 511
- vertex_ids: int32 [8, 196608], P(None, ('elem', 'clus')), may hold values from 0 to 24575, as said below
Outputs:
- applied: float32 [512, 196608], P(None, ('elem', 'clus'))
Inputs may be any that keep to these rules, and one draw needn't show every extreme that they name: `face_target`: No two faces of one device name the same slot, and on some device every slot is named. `vertex_ids`: the coarse vertices of the elements on elem index e lie in e * 256 to e * 256 + 2 * 256 - 1, taken modulo 24576.
All inputs are finite; a program needn't handle non-finite values.
Results may differ from a plain program's by a relative error of at most 0.0003.
Values sent between devices are 32-bit elements; how exact they have to be, the bound alone decides.
A program may use at most 32 MiB of HBM per device.

v0:
```python
import jax
import jax.numpy as jnp
from jax import lax
from jax.sharding import PartitionSpec as P

POINTS = 8
CAP_E = 128
CAP_C = 16
M_DEV = 512
NV_DEV = 256


highest = lax.Precision.HIGHEST


def extended(array, sides, width):
    for axis, dim in sides:
        peers, length = (lax.axis_size(axis), array.shape[dim])
        up = [(i, (i + 1) % peers) for i in range(peers)]
        down = [(j, i) for i, j in up]
        last = lax.slice_in_dim(array, length - width, length, axis=dim)
        initial = lax.slice_in_dim(array, 0, width, axis=dim)
        before = lax.ppermute(last, axis, up)
        after = lax.ppermute(initial, axis, down)
        array = jnp.concatenate([before, array, after], axis=dim)
    return array


def face_traces(nodal_block, points):
    element_cube = nodal_block.reshape(points, points, points, -1)
    far_index = points - 1
    slab_list = [
        element_cube[0],
        element_cube[far_index],
        element_cube[:, 0],
        element_cube[:, far_index],
        element_cube[:, :, 0],
        element_cube[:, :, far_index],
    ]
    return jnp.concatenate(slab_list, axis=2)


def face_maps(interp, face_level, points):
    identity = jnp.eye(points, dtype=jnp.float32)[:, :, None]
    first_one = interp[0][:, :, None]
    second_one = interp[1][:, :, None]
    level_row = face_level[None, None, :]
    left_map = jnp.where(level_row == 0, identity, jnp.where(level_row <= 2, first_one, second_one))
    right_map = jnp.where(
        level_row == 0, identity, jnp.where(level_row % 2 == 1, first_one, second_one)
    )
    return (left_map, right_map)


def project_traces(traces, left_map, right_map):
    partial_rows = jnp.einsum("xaf,abf->xbf", left_map, traces, precision=highest)
    return jnp.einsum("ybf,xbf->xyf", right_map, partial_rows, precision=highest)


def back_project(values, left_map, right_map):
    partial_rows = jnp.einsum("xaf,xyf->ayf", left_map, values, precision=highest)
    return jnp.einsum("ybf,ayf->abf", right_map, partial_rows, precision=highest)


def stiffness_apply(nodal_block, metric_block, derivative, points):
    element_cube = nodal_block.reshape(points, points, points, -1)
    metric_cube = metric_block.astype(jnp.float32).reshape(3, points, points, points, -1)
    grad_first = jnp.einsum("ai,ijke->ajke", derivative, element_cube, precision=highest)
    grad_second = jnp.einsum("bj,ijke->ibke", derivative, element_cube, precision=highest)
    grad_third = jnp.einsum("ck,ijke->ijce", derivative, element_cube, precision=highest)
    result = jnp.einsum("ai,ajke->ijke", derivative, metric_cube[0] * grad_first, precision=highest)
    result = result + jnp.einsum(
        "bj,ibke->ijke", derivative, metric_cube[1] * grad_second, precision=highest
    )
    result = result + jnp.einsum(
        "ck,ijce->ijke", derivative, metric_cube[2] * grad_third, precision=highest
    )
    return result


def corner_values(nodal_block, points):
    element_cube = nodal_block.reshape(points, points, points, -1)
    far_index = points - 1
    return jnp.stack(
        [
            element_cube[
                corner // 4 * far_index, corner // 2 % 2 * far_index, corner % 2 * far_index
            ]
            for corner in range(8)
        ]
    )


def finish_block(result_cube, back_faces, corner_fix, points):
    far_index = points - 1
    count_elems = result_cube.shape[-1]
    face_parts = back_faces.reshape(points, points, 6, count_elems)
    result_cube = result_cube.at[0].add(face_parts[:, :, 0])
    result_cube = result_cube.at[far_index].add(face_parts[:, :, 1])
    result_cube = result_cube.at[:, 0].add(face_parts[:, :, 2])
    result_cube = result_cube.at[:, far_index].add(face_parts[:, :, 3])
    result_cube = result_cube.at[:, :, 0].add(face_parts[:, :, 4])
    result_cube = result_cube.at[:, :, far_index].add(face_parts[:, :, 5])
    for corner in range(8):
        result_cube = result_cube.at[
            corner // 4 * far_index, corner // 2 % 2 * far_index, corner % 2 * far_index
        ].add(corner_fix[corner])
    return result_cube.reshape(points**3, count_elems)


def curve_swap(pair):
    return extended(pair, (("elem", 0),), 1)


def group_swap(columns):
    return lax.all_to_all(columns, "clus", split_axis=1, concat_axis=1, tiled=True)


def coarse_correction(nodal, vertex_ids, points):
    corner_vals = corner_values(nodal, points).reshape(-1)
    total_vertices = NV_DEV * lax.axis_size("elem")
    window_ids = jnp.mod(vertex_ids - lax.axis_index("elem") * NV_DEV, total_vertices)
    flat_ids = window_ids.reshape(-1)
    totals = jnp.zeros((2 * NV_DEV,), jnp.float32).at[flat_ids].add(corner_vals)
    counts = (
        jnp.zeros((2 * NV_DEV,), jnp.float32)
        .at[flat_ids]
        .add(jnp.ones(flat_ids.shape, jnp.float32))
    )
    totals, counts = lax.psum((totals, counts), "clus")
    stacked = jnp.stack([totals.reshape(2, NV_DEV), counts.reshape(2, NV_DEV)], axis=1)
    widened = extended(stacked, (("elem", 0),), 1)
    window = jnp.concatenate([widened[0] + widened[1], widened[2] + widened[3]], axis=1)
    coarse = window[0] / (1.0 + window[1])
    return coarse[window_ids]


def on_device(nodal, metric, derivative, interp, face_level, face_target, slot_mortar, vertex_ids):
    points = POINTS
    width_sq = points * points
    group_size = lax.axis_size("clus")
    slot_count = 2 * CAP_E + group_size * CAP_C
    left_map, right_map = face_maps(interp, face_level, points)
    projected = project_traces(face_traces(nodal, points), left_map, right_map)
    outgoing = (
        jnp.zeros((width_sq, M_DEV + slot_count), jnp.float32)
        .at[:, face_target]
        .add(projected.reshape(width_sq, -1))
    )
    edge_pair = jnp.stack(
        [outgoing[:, M_DEV : M_DEV + CAP_E], outgoing[:, M_DEV + CAP_E : M_DEV + 2 * CAP_E]]
    )
    arrived_pair = curve_swap(edge_pair)
    arrived_group = group_swap(outgoing[:, M_DEV + 2 * CAP_E :])
    incoming = jnp.concatenate([arrived_pair[0], arrived_pair[3], arrived_group], axis=1)
    mortar = outgoing[:, :M_DEV].at[:, slot_mortar].add(incoming)
    answers = mortar[:, slot_mortar]
    answer_pair = curve_swap(jnp.stack([answers[:, :CAP_E], answers[:, CAP_E : 2 * CAP_E]]))
    answer_group = group_swap(answers[:, 2 * CAP_E :])
    returned = jnp.concatenate([mortar, answer_pair[0], answer_pair[3], answer_group], axis=1)
    picked = returned[:, face_target].reshape(points, points, -1)
    back_faces = back_project(picked, left_map, right_map)
    result_cube = stiffness_apply(nodal, metric, derivative, points)
    corner_fix = coarse_correction(nodal, vertex_ids, points)
    return finish_block(result_cube, back_faces, corner_fix, points)


def solution(mesh):
    in_specs = (
        P(None, ("elem", "clus")),
        P(None, None, ("elem", "clus")),
        P(),
        P(),
        P(("elem", "clus")),
        P(("elem", "clus")),
        P(("elem", "clus")),
        P(None, ("elem", "clus")),
    )
    out_specs = P(None, ("elem", "clus"))
    return jax.shard_map(
        on_device, mesh=mesh, in_specs=in_specs, out_specs=out_specs, check_vma=False
    )
```

profile of v0, /device:TPU:1, one launch (start us, length us, event | category | flops | bytes accessed | tf_op | source)
XLA Modules:
  0.0 234.3 jit_solution(3746324955394271847)
XLA Ops:
  0.0 0.9 bitcast_dynamic-update-slice_fusion.2
  0.9 0.8 bitcast_dynamic-update-slice_fusion.1
  1.7 1.3 fusion.75
  3.0 0.8 fusion.50
  3.9 0.8 fusion.49
  4.8 4.0 %copy.56 = f32[8,8,1536]{0,1,2:T(8,128)} copy(f32[8,8,1536]{2,1,0:T(8,128)S(1)} %bitcast_dynamic-update-slice_fusion) | data formatting | bytes 786432 | tf_op jit(solution)/shard_map/concatenate | solution.py:40
  8.9 20.6 %fusion.5 = f32[1536,8,8]{1,2,0:T(8,128)S(1)} fusion(f32[8,8,1536]{0,1,2:T(8,128)} %copy.56, f32[8,8]{0,1:T(8,128)S(1)} %copy.37, f32[8,8]{0,1:T(8,128)S(1)} %copy.36, f32[8,8]{0,1:T(8,128)S(1)} %fusion.64, pred[1536]{0:T(1024)(128)(4,1)S(1)} %get-tuple-element.212, pred[1536]{0:T(1024)(128)(4,1)S(1)} %get-tuple-element.213), kind=kOutput, calls=%fused_computation.14 | convolution fusion | flops 9633792 | bytes 790272 | tf_op jit(solution)/shard_map/xaf,abf->xbf/dot_general | solution.py:56
  29.5 18.5 %fusion.26 = f32[8,8,1536]{1,0,2:T(8,128)} fusion(f32[8,8]{0,1:T(8,128)S(1)} %copy.37, f32[8,8]{0,1:T(8,128)S(1)} %copy.36, f32[8,8]{0,1:T(8,128)S(1)} %fusion.64, pred[1536]{0:T(1024)(128)(4,1)S(1)} %get-tuple-element.214, pred[1536]{0:T(1024)(128)(4,1)S(1)} %get-tuple-element.213, f32[1536,8,8]{1,2,0:T(8,128)S(1)} %fusion.5), kind=kOutput, calls=%fused_computation.35 | convolution fusion | flops 9633792 | bytes 790272 | tf_op jit(solution)/shard_map/ybf,xbf->xyf/dot_general | solution.py:57
  48.0 4.4 %copy.39 = f32[8,8,1536]{2,1,0:T(8,128)S(1)} copy(f32[8,8,1536]{1,0,2:T(8,128)} %fusion.26) | data formatting | bytes 786432 | tf_op jit(solution)/shard_map/ybf,xbf->xyf/transpose | solution.py:57
  52.5 0.3 copy.40
  52.8 8.9 %scatter_custom_fusion = f32[64,896]{0,1:T(8,128)S(1)} fusion(s32[1536]{0:T(1024)S(1)} %compare_select_fusion.2, f32[1536,64]{1,0:T(8,128)S(1)} %copy.40, f32[]{:T(128)} %constant.454.clone.1), kind=kCustom, calls=%fused_computation.48 | custom fusion | flops 98304 | bytes 229380 | tf_op jit(solution)/shard_map/scatter-add | solution.py:148
  61.7 0.7 reshape.681
  62.4 13.7 %all-to-all-start = ((f32[8,1,1024]{2,1,0:T(1,128)}), f32[8,1,1024]{2,1,0:T(1,128)S(1)}, u32[]{:S(2)}, u32[]{:S(2)}) async-start(f32[8,1,1024]{2,1,0:T(1,128)} %reshape.681), calls=%async_computation | async-start | bytes 65536 | tf_op jit(solution)/shard_map/all_to_all | solution.py:116
  76.1 1.9 collective-permute-start
  78.1 9.4 %collective-permute-start.1 = (f32[1,64,128]{1,2,0:T(8,128)S(1)}, f32[1,64,128]{1,2,0:T(8,128)S(1)}, u32[]{:S(2)}, u32[]{:S(2)}) collective-permute-start(f32[1,64,128]{1,2,0:T(8,128)S(1)} %get-tuple-element.192), channel_id=1, source_target_pairs={{8,0},{16,8},{24,16},{32,24},{40,32},{48,40},{56,48},{64,56},{72,6... | collective-permute-start | bytes 98312 | tf_op jit(solution)/shard_map/ppermute | solution.py:24
  87.7 14.7 %scatter_custom_fusion.2 = f32[512]{0:T(512)S(1)} fusion(s32[2048]{0:T(1024)S(1)} %bitcast.206, f32[2048]{0:T(1024)S(1)} %bitcast.205, f32[]{:T(128)} %constant.454.clone.1), kind=kCustom, calls=%fused_computation.143 | custom fusion | flops 2048 | bytes 2052 | tf_op jit(solution)/shard_map/scatter-add | solution.py:124
  102.3 14.7 %scatter_custom_fusion.3 = f32[512]{0:T(512)S(1)} fusion(s32[2048]{0:T(1024)S(1)} %bitcast.207, f32[2048]{0:T(1024)S(1)} %broadcast.281, f32[]{:T(128)} %constant.454.clone.1), kind=kCustom, calls=%fused_computation.141 | custom fusion | flops 2048 | bytes 2052 | tf_op jit(solution)/shard_map/scatter-add | solution.py:128
  117.0 12.5 %all-reduce = (f32[2,1,256]{2,1,0:T(1,128)S(1)}, f32[2,1,256]{2,1,0:T(1,128)S(1)}) all-reduce(f32[2,1,256]{2,1,0:T(1,128)S(1)} %bitcast.203, f32[2,1,256]{2,1,0:T(1,128)S(1)} %bitcast.204), channel_id=1, replica_groups=mesh['elem'=96,'clus'=8] {'clus'}, use_global_device_ids=true, to_apply=%region_3.4 | all-reduce | flops 1024 | bytes 8192 | tf_op jit(solution)/shard_map/psum | solution.py:130
  129.5 3.6 %collective-permute-start.5 = (f32[1,2,256]{2,1,0:T(2,128)S(1)}, f32[1,2,256]{2,1,0:T(2,128)S(1)}, u32[]{:S(2)}, u32[]{:S(2)}) collective-permute-start(f32[1,2,256]{2,1,0:T(2,128)S(1)} %pad_maximum_fusion.2), channel_id=1, source_target_pairs={{8,0},{16,8},{24,16},{32,24},{40,32},{48,40},{56,48},{64,56},{72,6... | collective-permute-start | bytes 6152 | tf_op jit(solution)/shard_map/ppermute | solution.py:24
  133.2 0.1 fusion.74
  133.3 0.6 fusion.35
  133.9 0.6 fusion.56
  134.5 0.8 fusion.34
  135.3 0.6 fusion.58
  135.9 1.1 convolution_multiply_fusion
  137.0 1.1 fusion.33
  138.2 1.9 collective-permute-start.4
  140.2 5.7 %collective-permute-done.4 = f32[1,2,256]{2,1,0:T(2,128)S(1)} collective-permute-done((f32[1,2,256]{2,1,0:T(2,128)S(1)}, f32[1,2,256]{2,1,0:T(2,128)S(1)}, u32[]{:S(2)}, u32[]{:S(2)}) %collective-permute-start.4) | collective-permute-done | bytes 2080 | tf_op jit(solution)/shard_map/ppermute | solution.py:23
  145.9 13.2 %gather_fusion.2 = f32[2048]{0:T(1024)S(1)} fusion(f32[512]{0:T(512)S(1)} %bitcast.176, s32[2048]{0:T(1024)S(1)} %broadcast_clamp_fusion), kind=kCustom, calls=%fused_computation.2 | custom fusion | bytes 24576 | tf_op jit(solution)/shard_map/gather | solution.py:135
  159.1 0.5 broadcast.306
  159.6 0.7 reduce.28
  160.4 2.8 %scatter_custom_fusion.1 = f32[64,512]{0,1:T(8,128)S(1)} fusion(f32[64,512]{0,1:T(8,128)S(1)} %slice-done, s32[384]{0:T(512)S(1)} %compare_select_fusion.3, f32[64,128]{0,1:T(8,128)S(1)} %bitcast.193, f32[]{:T(128)} %constant.470, f32[64,128]{0,1:T(8,128)S(1)} %bitcast.199, f32[64,128]{0,1:T(8,128)S(1)} %bitcast.198), kind=kCustom, calls=%fused_computation.51 | custom fusion | flops 73728 | bytes 327684 | tf_op jit(solution)/shard_map/scatter-add | solution.py:156
  163.2 1.1 gather_fusion
  164.3 0.7 reshape.683
  165.0 7.3 %all-to-all-start.1 = ((f32[8,1,1024]{2,1,0:T(1,128)}), f32[8,1,1024]{2,1,0:T(1,128)S(1)}, u32[]{:S(2)}, u32[]{:S(2)}) async-start(f32[8,1,1024]{2,1,0:T(1,128)} %reshape.683), calls=%async_computation.1 | async-start | bytes 65536 | tf_op jit(solution)/shard_map/all_to_all | solution.py:116
  172.4 1.9 collective-permute-start.2
  174.3 6.9 %collective-permute-start.3 = (f32[1,64,128]{1,2,0:T(8,128)S(1)}, f32[1,64,128]{1,2,0:T(8,128)S(1)}, u32[]{:S(2)}, u32[]{:S(2)}) collective-permute-start(f32[1,64,128]{1,2,0:T(8,128)S(1)} %get-tuple-element.200), channel_id=1, source_target_pairs={{8,0},{16,8},{24,16},{32,24},{40,32},{48,40},{56,48},{64,56},{72,6... | collective-permute-start | bytes 98312 | tf_op jit(solution)/shard_map/ppermute | solution.py:24
  181.2 0.7 reduce.29
  182.0 0.3 collective-permute-done.3
  182.3 2.6 %gather_fusion.1 = f32[1536,64]{1,0:T(8,128)S(1)} fusion(f32[64,896]{0,1:T(8,128)S(1)} %pad_maximum_fusion, s32[2048]{0:T(1024)S(1)} %pad_clamp_fusion), kind=kCustom, calls=%fused_computation.1 | custom fusion | bytes 792576 | tf_op jit(solution)/shard_map/gather | solution.py:161
  184.9 0.2 copy.41
  185.2 4.0 %copy.58 = f32[8,8,1536]{0,1,2:T(8,128)} copy(f32[8,8,1536]{2,1,0:T(8,128)S(1)} %bitcast.190) | data formatting | bytes 786432 | tf_op jit(solution)/shard_map/reshape | solution.py:161
  189.2 18.7 %fusion.4 = f32[1536,8,8]{1,2,0:T(8,128)S(1)} fusion(f32[8,8,1536]{0,1,2:T(8,128)} %copy.58, f32[8,8]{0,1:T(8,128)S(1)} %copy.37, f32[8,8]{0,1:T(8,128)S(1)} %copy.36, f32[8,8]{0,1:T(8,128)S(1)} %fusion.64, pred[1536]{0:T(1024)(128)(4,1)S(1)} %get-tuple-element.212, pred[1536]{0:T(1024)(128)(4,1)S(1)} %get-tuple-element.213), kind=kOutput, calls=%fused_computation.13 | convolution fusion | flops 9633792 | bytes 790272 | tf_op jit(solution)/shard_map/xaf,xyf->ayf/dot_general | solution.py:61
  207.9 18.6 %fusion.29 = f32[8,8,1536]{0,1,2:T(8,128)} fusion(f32[8,8]{0,1:T(8,128)S(1)} %copy.37, f32[8,8]{0,1:T(8,128)S(1)} %copy.36, f32[8,8]{0,1:T(8,128)S(1)} %fusion.64, pred[1536]{0:T(1024)(128)(4,1)S(1)} %get-tuple-element.214, pred[1536]{0:T(1024)(128)(4,1)S(1)} %get-tuple-element.213, f32[1536,8,8]{1,2,0:T(8,128)S(1)} %fusion.4), kind=kOutput, calls=%fused_computation.36 | convolution fusion | flops 9633792 | bytes 790272 | tf_op jit(solution)/shard_map/ybf,ayf->abf/dot_general | solution.py:62
  226.4 4.4 %copy.42 = f32[8,8,1536]{2,1,0:T(8,128)S(1)} copy(f32[8,8,1536]{0,1,2:T(8,128)} %fusion.29) | data formatting | bytes 786432 | tf_op jit(solution)/shard_map/ybf,ayf->abf/transpose | solution.py:62
  231.0 0.8 scatter-add.76
  231.9 0.8 scatter-add.79
  233.4 1.0 copy.49
  (79 shorter events, 1.3 us)
Async XLA Ops:
  0.0 133.3 %copy-start = (f32[8,8]{1,0:T(8,128)S(1)}, f32[8,8]{1,0:T(8,128)}, u32[]{:S(2)}) copy-start(f32[8,8]{1,0:T(8,128)} %param.38) | copy-start | bytes 772
  0.0 8.7 %copy-start.5 = (s32[1536]{0:T(1024)S(1)}, s32[1536]{0:T(1024)}, u32[]{:S(2)}) copy-start(s32[1536]{0:T(1024)} %param.40) | copy-start | bytes 18436
  0.0 8.7 %copy-start.6 = (f32[2,8,8]{2,1,0:T(8,128)S(1)}, f32[2,8,8]{2,1,0:T(8,128)}, u32[]{:S(2)}) copy-start(f32[2,8,8]{2,1,0:T(8,128)} %param.39) | copy-start | bytes 1540
  48.0 4.8 %copy-start.7 = (s32[1536]{0:T(1024)S(1)}, s32[1536]{0:T(1024)}, u32[]{:S(2)}) copy-start(s32[1536]{0:T(1024)} %param.41) | copy-start | bytes 18436
  48.0 39.5 %copy-start.1 = (f32[512,256]{1,0:T(8,128)S(1)}, f32[512,256]{1,0:T(8,128)}, u32[]{:S(2)}) copy-start(f32[512,256]{1,0:T(8,128)} %param.36) | copy-start | bytes 1572868
  48.0 39.6 %copy-start.4 = (s32[8,256]{1,0:T(8,128)S(1)}, s32[8,256]{1,0:T(8,128)}, u32[]{:S(2)}) copy-start(s32[8,256]{1,0:T(8,128)} %param.43) | copy-start | bytes 24580
  48.0 85.1 %copy-start.8 = (s32[384]{0:T(512)S(1)}, s32[384]{0:T(512)}, u32[]{:S(2)}) copy-start(s32[384]{0:T(512)} %param.42) | copy-start | bytes 4612
  48.0 85.1 %copy-start.3 = (bf16[3,512,256]{2,1,0:T(8,128)(2,1)S(1)}, bf16[3,512,256]{2,1,0:T(8,128)(2,1)}, u32[]{:S(2)}) copy-start(bf16[3,512,256]{2,1,0:T(8,128)(2,1)} %param.37) | copy-start | bytes 2359300
  61.6 78.5 %copy-start.2 = (f32[64,896]{0,1:T(8,128)}, f32[64,896]{0,1:T(8,128)S(1)}, u32[]{:S(2)}) copy-start(f32[64,896]{0,1:T(8,128)S(1)} %scatter_custom_fusion) | copy-start | bytes 688132
  62.4 96.7 %all-to-all-start = ((f32[8,1,1024]{2,1,0:T(1,128)}), f32[8,1,1024]{2,1,0:T(1,128)S(1)}, u32[]{:S(2)}, u32[]{:S(2)}) async-start(f32[8,1,1024]{2,1,0:T(1,128)} %reshape.681), calls=%async_computation | async-start | bytes 65536 | tf_op jit(solution)/shard_map/all_to_all | solution.py:116
  76.1 84.3 %collective-permute-start = (f32[1,64,128]{1,2,0:T(8,128)S(1)}, f32[1,64,128]{1,2,0:T(8,128)S(1)}, u32[]{:S(2)}, u32[]{:S(2)}) collective-permute-start(f32[1,64,128]{1,2,0:T(8,128)S(1)} %get-tuple-element.190), channel_id=1, source_target_pairs={{0,8},{8,16},{16,24},{24,32},{32,40},{40,48},{48,56},{56,64},{64,7... | collective-permute-start | bytes 98312 | tf_op jit(solution)/shard_map/ppermute | solution.py:23
  78.1 82.3 %collective-permute-start.1 = (f32[1,64,128]{1,2,0:T(8,128)S(1)}, f32[1,64,128]{1,2,0:T(8,128)S(1)}, u32[]{:S(2)}, u32[]{:S(2)}) collective-permute-start(f32[1,64,128]{1,2,0:T(8,128)S(1)} %get-tuple-element.192), channel_id=1, source_target_pairs={{8,0},{16,8},{24,16},{32,24},{40,32},{48,40},{56,48},{64,56},{72,6... | collective-permute-start | bytes 98312 | tf_op jit(solution)/shard_map/ppermute | solution.py:24
  129.5 8.7 %collective-permute-start.5 = (f32[1,2,256]{2,1,0:T(2,128)S(1)}, f32[1,2,256]{2,1,0:T(2,128)S(1)}, u32[]{:S(2)}, u32[]{:S(2)}) collective-permute-start(f32[1,2,256]{2,1,0:T(2,128)S(1)} %pad_maximum_fusion.2), channel_id=1, source_target_pairs={{8,0},{16,8},{24,16},{32,24},{40,32},{48,40},{56,48},{64,56},{72,6... | collective-permute-start | bytes 6152 | tf_op jit(solution)/shard_map/ppermute | solution.py:24
  138.2 7.6 %collective-permute-start.4 = (f32[1,2,256]{2,1,0:T(2,128)S(1)}, f32[1,2,256]{2,1,0:T(2,128)S(1)}, u32[]{:S(2)}, u32[]{:S(2)}) collective-permute-start(f32[1,2,256]{2,1,0:T(2,128)S(1)} %get-tuple-element.176), channel_id=1, source_target_pairs={{0,8},{8,16},{16,24},{24,32},{32,40},{40,48},{48,56},{56,64},{64,7... | collective-permute-start | bytes 6152 | tf_op jit(solution)/shard_map/ppermute | solution.py:23
  140.1 20.3 %slice-start = ((f32[64,896]{0,1:T(8,128)}), f32[64,512]{0,1:T(8,128)S(1)}, s32[]{:S(2)}) async-start(f32[64,896]{0,1:T(8,128)} %copy-done.2), calls=%async_computation.2 | async-start | bytes 524288 | tf_op jit(solution)/shard_map/slice | solution.py:156
  165.0 16.2 %all-to-all-start.1 = ((f32[8,1,1024]{2,1,0:T(1,128)}), f32[8,1,1024]{2,1,0:T(1,128)S(1)}, u32[]{:S(2)}, u32[]{:S(2)}) async-start(f32[8,1,1024]{2,1,0:T(1,128)} %reshape.683), calls=%async_computation.1 | async-start | bytes 65536 | tf_op jit(solution)/shard_map/all_to_all | solution.py:116
  172.4 9.6 %collective-permute-start.2 = (f32[1,64,128]{1,2,0:T(8,128)S(1)}, f32[1,64,128]{1,2,0:T(8,128)S(1)}, u32[]{:S(2)}, u32[]{:S(2)}) collective-permute-start(f32[1,64,128]{1,2,0:T(8,128)S(1)} %get-tuple-element.199), channel_id=1, source_target_pairs={{0,8},{8,16},{16,24},{24,32},{32,40},{40,48},{48,56},{56,64},{64,7... | collective-permute-start | bytes 98312 | tf_op jit(solution)/shard_map/ppermute | solution.py:23
  174.3 8.0 %collective-permute-start.3 = (f32[1,64,128]{1,2,0:T(8,128)S(1)}, f32[1,64,128]{1,2,0:T(8,128)S(1)}, u32[]{:S(2)}, u32[]{:S(2)}) collective-permute-start(f32[1,64,128]{1,2,0:T(8,128)S(1)} %get-tuple-element.200), channel_id=1, source_target_pairs={{8,0},{16,8},{24,16},{32,24},{40,32},{48,40},{56,48},{64,56},{72,6... | collective-permute-start | bytes 98312 | tf_op jit(solution)/shard_map/ppermute | solution.py:24
where the time goes:
time: 235 us; the launch traced here: 234 us
  matrix products  81.1 us (35%)
  starting transfers between devices  46.8 us (20%)
  local copies, waits for them, and re-layouts  44.5 us (19%)
  other arithmetic  42.8 us (18%)
  blocking collectives  12.5 us (5%)
  waiting for transfers between devices  5.97 us (3%)
    all_to_all x2, starting transfers between devices, group_swap(): lax.all_to_all(columns, 'clus', split_axis=1, concat_axis=1, tiled=True)  21.1 us
    dot_general x1, matrix products, project_traces(): jnp.einsum('xaf,abf->xbf', left_map, traces, precision=highest)  20.6 us
    ppermute x3, starting transfers between devices, extended(): after = lax.ppermute(initial, axis, down)  20 us
    dot_general x1, matrix products, back_project(): jnp.einsum('xaf,xyf->ayf', left_map, values, precision=highest)  18.7 us
    dot_general x1, matrix products, back_project(): jnp.einsum('ybf,ayf->abf', right_map, partial_rows, precision=highest)  18.6 us
    dot_general x1, matrix products, project_traces(): jnp.einsum('ybf,xbf->xyf', right_map, partial_rows, precision=highest)  18.5 us
    scatter-add x1, other arithmetic, coarse_correction(): counts = jnp.zeros((2 * NV_DEV,), jnp.float32).at[flat_ids].add(jnp.ones(...  14.7 us
    scatter-add x1, other arithmetic, coarse_correction(): totals = jnp.zeros((2 * NV_DEV,), jnp.float32).at[flat_ids].add(corner_vals)  14.7 us
  transfers between devices with their start and end apart: 8, of which 2 were waited for; matrix products, arithmetic and copies ran while one was open for 21% of the time, Pallas kernels for 0%

commit v1 on v0

v1 whole, which is shorter than its diff:
```python
import functools

import jax
import jax.numpy as jnp
from jax import lax
from jax.experimental import pallas as pl
from jax.experimental.pallas import tpu as pltpu
from jax.sharding import PartitionSpec as P

CAP_E = 128
CAP_C = 16
GROUP = 8
M_DEV = 512
SLOTS = 2 * CAP_E + GROUP * CAP_C
COLS = M_DEV + SLOTS
NV_DEV = 256
E_DEV = 256
FACES = 6 * E_DEV
NODES = 512
MESH = pl.DeviceIdType.MESH
F32 = jnp.float32
BF16 = jnp.bfloat16

NT = (((1,), (1,)), ((), ()))
NN = (((1,), (0,)), ((), ()))


def mm(a, b, dims=NN):
    return lax.dot_general(a, b, dims, preferred_element_type=F32)


def split(x):
    hi = x.astype(BF16)
    return hi, (x - hi.astype(F32)).astype(BF16)


def stacked(x):
    hi, lo = split(x)
    return jnp.concatenate([hi, lo, hi], axis=0)


def halves(x):
    return x[:64] + x[64:]


def iota(shape, axis):
    return lax.broadcasted_iota(jnp.int32, shape, axis)


def three_terms(full):
    hi = full.astype(BF16).astype(F32)
    lane = iota(full.shape, 1)
    return jnp.where(lane < 128, hi, full - hi).astype(BF16)


def kernel(
    n_elem,
    u_hbm,
    met_hbm,
    ma_hbm,
    mb_hbm,
    lvl_hbm,
    tgt_hbm,
    slot_hbm,
    vid_hbm,
    out,
    u,
    met,
    ma,
    mb,
    lvl,
    tgt,
    slot,
    vid,
    pick,
    pick2,
    corner_hot,
    proj,
    own,
    picked,
    grad0,
    acc,
    send_e,
    send_g,
    recv_e,
    recv_g,
    send_e2,
    send_g2,
    recv_e2,
    recv_g2,
    in_sem,
    se_sem,
    re_sem,
    sg_sem,
    rg_sem,
    se2_sem,
    re2_sem,
    sg2_sem,
    rg2_sem,
):
    e = lax.axis_index("elem")
    c = lax.axis_index("clus")
    nxt = lax.rem(e + 1, n_elem)
    prv = lax.rem(e + n_elem - 1, n_elem)

    loads = [
        pltpu.make_async_copy(src, dst, in_sem.at[n])
        for n, (src, dst) in enumerate(
            [
                (tgt_hbm, tgt),
                (u_hbm.at[:, 0:128], u.at[0]),
                (u_hbm.at[:, 128:256], u.at[1]),
                (ma_hbm, ma),
                (mb_hbm, mb),
                (lvl_hbm, lvl),
                (vid_hbm, vid),
                (slot_hbm, slot),
                (met_hbm, met),
            ]
        )
    ]
    for load in loads:
        load.start()

    def node_rows(ref, place):
        return jnp.concatenate([ref[0, place, :], ref[1, place, :]], axis=1)

    def add_rows(place, value):
        for side in range(2):
            acc[side, place, :] = acc[side, place, :] + value[:, 128 * side : 128 * side + 128]

    barrier = pltpu.get_barrier_semaphore()
    for peer in (nxt, prv):
        pl.semaphore_signal(barrier, inc=1, device_id={"elem": peer}, device_id_type=MESH)
    for k in range(1, GROUP):
        peer = lax.rem(c + k, GROUP)
        pl.semaphore_signal(barrier, inc=1, device_id={"clus": peer}, device_id_type=MESH)

    loads[0].wait()
    rows = iota((COLS, 128), 0)
    for b in range(FACES // 128):
        hot = jnp.where(rows == tgt[b : b + 1, :], 1.0, 0.0).astype(BF16)
        pick[:, b * 128 : (b + 1) * 128] = hot

    loads[3].wait()
    loads[4].wait()

    def kron(first, second):
        return jnp.concatenate(
            [
                jnp.broadcast_to(ma[8 * first + x : 8 * first + x + 1, :], (8, 192))
                * mb[8 * second : 8 * second + 8, :]
                for x in range(8)
            ],
            axis=0,
        )

    def first_kron(which):
        full = jnp.concatenate(
            [
                jnp.broadcast_to(ma[8 * which + x : 8 * which + x + 1, :], (8, 192))
                for x in range(8)
            ],
            axis=0,
        )
        keep = (iota((64, 192), 0) & 7) == (iota((64, 192), 1) & 7)
        return jnp.where(keep, full, 0.0)

    def second_kron(which):
        full = jnp.concatenate([mb[8 * which : 8 * which + 8, :]] * 8, axis=0)
        keep = (iota((64, 192), 0) >> 3) == ((iota((64, 192), 1) & 63) >> 3)
        return jnp.where(keep, full, 0.0)

    pairs = [(0, 0), (0, 1), (1, 0), (1, 1)]
    forth = three_terms(jnp.concatenate([kron(r, s) for r, s in pairs], axis=0))

    loads[1].wait()
    loads[2].wait()
    loads[5].wait()
    for f in range(6):
        if f == 0:
            trace = node_rows(u, slice(0, 64))
        elif f == 1:
            trace = node_rows(u, slice(448, 512))
        elif f == 2:
            trace = jnp.concatenate([node_rows(u, slice(64 * i, 64 * i + 8)) for i in range(8)], axis=0)
        elif f == 3:
            trace = jnp.concatenate(
                [node_rows(u, slice(64 * i + 56, 64 * i + 64)) for i in range(8)], axis=0
            )
        else:
            first = 0 if f == 4 else 7
            trace = node_rows(u, pl.ds(first, 64, stride=8))
        level = jnp.concatenate([lvl[2 * f : 2 * f + 1, :], lvl[2 * f + 1 : 2 * f + 2, :]], axis=1)
        level = jnp.broadcast_to(level, (64, E_DEV))
        every = mm(forth, stacked(trace))
        chosen = trace
        for n in range(4):
            chosen = jnp.where(level == n + 1, every[64 * n : 64 * n + 64], chosen)
        hi, lo = split(chosen)
        proj[0:64, f * 256 : (f + 1) * 256] = hi
        proj[64:128, f * 256 : (f + 1) * 256] = lo

    loads[6].wait()
    away = vid[...] - e * NV_DEV
    total_vertices = n_elem * NV_DEV
    window = jnp.where(away < 0, away + total_vertices, away)
    high = window >> 6
    low = window & 63
    sums = jnp.zeros((32, 128), F32)
    eight = iota((8, E_DEV), 0)
    lanes_rows = iota((128, E_DEV), 0) - 64
    for corner in range(8):
        row = 7 * (64 * (corner // 4) + 8 * (corner // 2 % 2) + corner % 2)
        value = jnp.broadcast_to(node_rows(u, slice(row, row + 1)), (8, E_DEV))
        hi = value.astype(BF16).astype(F32)
        here = eight == high[corner : corner + 1, :]
        parts = [
            jnp.where(here, hi, 0.0),
            jnp.where(here, value - hi, 0.0),
            jnp.where(here, 1.0, 0.0),
            jnp.zeros((8, E_DEV), F32),
        ]
        hot = jnp.where(lanes_rows == low[corner : corner + 1, :], 1.0, 0.0).astype(BF16)
        corner_hot[:, corner * 256 : (corner + 1) * 256] = hot
        sums = sums + mm(jnp.concatenate(parts, axis=0).astype(BF16), hot, NT)
    local = jnp.concatenate([sums[0:8] + sums[8:16], sums[16:24]], axis=0)

    leaving = halves(mm(proj[...], pick[M_DEV:COLS, :], NT))
    send_e[0] = leaving[:, 0:128]
    send_e[1] = leaving[:, 128:256]
    turned = jnp.concatenate([leaving[:, 256:384], jnp.zeros((64, 128), F32)], axis=0).T
    send_g[...] = turned + jnp.concatenate([local] * GROUP, axis=0)

    def edge_copies(src, dst, ssem, rsem):
        return [
            pltpu.make_async_remote_copy(
                src.at[way],
                dst.at[1 - way],
                ssem.at[way],
                rsem.at[1 - way],
                device_id={"elem": peer},
                device_id_type=MESH,
            )
            for way, peer in ((0, prv), (1, nxt))
        ]

    def group_copies(src, dst, ssem, rsem, rows):
        copies = []
        for k in range(1, GROUP):
            peer = lax.rem(c + k, GROUP)
            copies.append(
                pltpu.make_async_remote_copy(
                    src.at[pl.ds(pl.multiple_of(peer * rows, rows), rows), :],
                    dst.at[pl.ds(pl.multiple_of(c * rows, rows), rows), :],
                    ssem.at[k - 1],
                    rsem.at[k - 1],
                    device_id={"clus": peer},
                    device_id_type=MESH,
                )
            )
        return copies

    pl.semaphore_wait(barrier, GROUP + 1)
    first_round = edge_copies(send_e, recv_e, se_sem, re_sem)
    first_round += group_copies(send_g, recv_g, sg_sem, rg_sem, CAP_C)
    for copy in first_round:
        copy.start()
    mine = pl.ds(pl.multiple_of(c * CAP_C, CAP_C), CAP_C)
    recv_g[mine, :] = send_g[mine, :]

    own[...] = halves(mm(proj[...], pick[0:M_DEV, :], NT))
    loads[7].wait()
    rows2 = iota((M_DEV, 128), 0)
    for b in range(SLOTS // 128):
        hot = jnp.where(rows2 == slot[b : b + 1, :], 1.0, 0.0).astype(BF16)
        pick2[:, b * 128 : (b + 1) * 128] = hot

    loads[8].wait()
    d_first = first_kron(2)
    d_second = second_kron(2)
    fore12 = three_terms(jnp.concatenate([d_first, d_second], axis=0))
    fore0 = fore12[0:64]
    t_first = three_terms(first_kron(5))
    t_second = three_terms(second_kron(5))
    for j in range(8):
        part = jnp.concatenate(
            [node_rows(u, slice(64 * i + 8 * j, 64 * i + 8 * j + 8)) for i in range(8)], axis=0
        )
        grad = mm(fore0, stacked(part))
        for i in range(8):
            grad0[64 * i + 8 * j : 64 * i + 8 * j + 8, :] = grad[8 * i : 8 * i + 8]
    for i in range(8):
        block = slice(64 * i, 64 * i + 64)
        grad = mm(fore12, stacked(node_rows(u, block)))
        flow1 = met[1, block, :].astype(F32) * grad[0:64]
        flow2 = met[2, block, :].astype(F32) * grad[64:128]
        grad0[block, :] = met[0, block, :].astype(F32) * grad0[block, :]
        back = mm(t_first, stacked(flow1)) + mm(t_second, stacked(flow2))
        acc[0, block, :] = back[:, 0:128]
        acc[1, block, :] = back[:, 128:256]
    for j in range(8):
        part = jnp.concatenate(
            [grad0[64 * i + 8 * j : 64 * i + 8 * j + 8, :] for i in range(8)], axis=0
        )
        back = mm(t_first, stacked(part))
        for i in range(8):
            add_rows(slice(64 * i + 8 * j, 64 * i + 8 * j + 8), back[8 * i : 8 * i + 8])
    backward = three_terms(jnp.concatenate([kron(r + 3, s + 3) for r, s in pairs], axis=0))

    for copy in first_round:
        copy.wait()
    group_in = recv_g[...]
    arrived = jnp.concatenate([recv_e[0], recv_e[1], group_in.T[0:64]], axis=1)
    hi, lo = split(arrived)
    mortar = own[...] + halves(mm(jnp.concatenate([hi, lo], axis=0), pick2[...], NT))
    hi, lo = split(mortar)
    mortar2 = jnp.concatenate([hi, lo], axis=0)
    answers = halves(mm(mortar2, pick2[...]))
    coarse_sum = group_in[0:16]
    for i in range(1, GROUP):
        coarse_sum = coarse_sum + group_in[16 * i : 16 * i + 16]
    send_e2[0, 0:64, :] = answers[:, 0:128]
    send_e2[1, 0:64, :] = answers[:, 128:256]
    send_e2[0, 64:80, :] = coarse_sum
    send_e2[1, 64:80, :] = coarse_sum
    send_g2[...] = jnp.concatenate([answers[:, 256:384], jnp.zeros((64, 128), F32)], axis=0).T
    second_round = edge_copies(send_e2, recv_e2, se2_sem, re2_sem)
    second_round += group_copies(send_g2, recv_g2, sg2_sem, rg2_sem, CAP_C)
    for copy in second_round:
        copy.start()
    recv_g2[mine, :] = send_g2[mine, :]

    picked[...] = halves(mm(mortar2, pick[0:M_DEV, :]))

    for copy in second_round:
        copy.wait()
    returned = jnp.concatenate([recv_e2[0, 0:64, :], recv_e2[1, 0:64, :], recv_g2[...].T[0:64]], axis=1)
    hi, lo = split(returned)
    returned2 = jnp.concatenate([hi, lo], axis=0)
    before = recv_e2[0, 64:80, :]
    after = recv_e2[1, 64:80, :]

    def widen(mid, left, right):
        near = jnp.where(
            iota((8, 128), 0) < 4, pltpu.roll(left, 4, 0), pltpu.roll(right, 4, 0)
        )
        return jnp.where(iota((8, 128), 1) >= 64, mid + near, 0.0)

    totals = widen(coarse_sum[0:8], before[0:8], after[0:8])
    counts = widen(coarse_sum[8:16], before[8:16], after[8:16])
    coarse = totals / (1.0 + counts)
    coarse_hi = coarse.astype(BF16).astype(F32)
    coarse2 = jnp.concatenate([coarse_hi, coarse - coarse_hi], axis=0).astype(BF16)
    spread = mm(coarse2, corner_hot[...])
    spread = spread[0:8] + spread[8:16]

    for f in range(6):
        span = slice(f * 256, (f + 1) * 256)
        value = picked[:, span] + halves(mm(returned2, pick[M_DEV:COLS, span]))
        level = jnp.concatenate([lvl[2 * f : 2 * f + 1, :], lvl[2 * f + 1 : 2 * f + 2, :]], axis=1)
        level = jnp.broadcast_to(level, (64, E_DEV))
        every = mm(backward, stacked(value))
        chosen = value
        for n in range(4):
            chosen = jnp.where(level == n + 1, every[64 * n : 64 * n + 64], chosen)
        if f < 2:
            add_rows(slice(448 * f, 448 * f + 64), chosen)
        elif f < 4:
            for i in range(8):
                first = 64 * i + 56 * (f - 2)
                add_rows(slice(first, first + 8), chosen[8 * i : 8 * i + 8])
        else:
            add_rows(pl.ds(7 * (f - 4), 64, stride=8), chosen)
    for corner in range(8):
        row = 7 * (64 * (corner // 4) + 8 * (corner // 2 % 2) + corner % 2)
        here = eight == high[corner : corner + 1, :]
        fix = jnp.where(here, spread[:, corner * 256 : (corner + 1) * 256], 0.0)
        add_rows(slice(row, row + 1), jnp.sum(fix, axis=0, keepdims=True))
    out[:, 0:128] = acc[0]
    out[:, 128:256] = acc[1]


def on_device(n_elem, nodal, metric, derivative, interp, face_level, face_target, slot_mortar, vertex_ids):
    mats = jnp.concatenate([interp, derivative[None]], axis=0)
    mats = jnp.concatenate([mats, mats.transpose(0, 2, 1)], axis=0).reshape(48, 8)
    first = jnp.broadcast_to(mats[:, None, :, None], (48, 3, 8, 8)).reshape(48, 192)
    second = jnp.broadcast_to(mats[:, None, None, :], (48, 3, 8, 8)).reshape(48, 192)
    anywhere = pl.BlockSpec(memory_space=pl.ANY)
    dma = pltpu.SemaphoreType.DMA
    return pl.pallas_call(
        functools.partial(kernel, n_elem),
        out_shape=jax.ShapeDtypeStruct((NODES, E_DEV), F32),
        in_specs=[anywhere] * 8,
        out_specs=pl.BlockSpec(memory_space=pltpu.VMEM),
        scratch_shapes=[
            pltpu.VMEM((2, NODES, 128), F32),
            pltpu.VMEM((3, NODES, E_DEV), BF16),
            pltpu.VMEM((48, 192), F32),
            pltpu.VMEM((48, 192), F32),
            pltpu.VMEM((12, 128), jnp.int32),
            pltpu.VMEM((12, 128), jnp.int32),
            pltpu.VMEM((3, 128), jnp.int32),
            pltpu.VMEM((8, E_DEV), jnp.int32),
            pltpu.VMEM((COLS, FACES), BF16),
            pltpu.VMEM((M_DEV, SLOTS), BF16),
            pltpu.VMEM((128, 8 * E_DEV), BF16),
            pltpu.VMEM((128, FACES), BF16),
            pltpu.VMEM((64, M_DEV), F32),
            pltpu.VMEM((64, FACES), F32),
            pltpu.VMEM((NODES, E_DEV), F32),
            pltpu.VMEM((2, NODES, 128), F32),
            pltpu.VMEM((2, 64, 128), F32),
            pltpu.VMEM((128, 128), F32),
            pltpu.VMEM((2, 64, 128), F32),
            pltpu.VMEM((128, 128), F32),
            pltpu.VMEM((2, 80, 128), F32),
            pltpu.VMEM((128, 128), F32),
            pltpu.VMEM((2, 80, 128), F32),
            pltpu.VMEM((128, 128), F32),
            dma((9,)),
            dma((2,)),
            dma((2,)),
            dma((7,)),
            dma((7,)),
            dma((2,)),
            dma((2,)),
            dma((7,)),
            dma((7,)),
        ],
        compiler_params=pltpu.CompilerParams(
            collective_id=0, has_side_effects=True, vmem_limit_bytes=48 * 1024 * 1024
        ),
    )(
        nodal,
        metric,
        first,
        second,
        face_level.reshape(12, 128),
        face_target.reshape(12, 128),
        slot_mortar.reshape(3, 128),
        vertex_ids,
    )


def solution(mesh):
    in_specs = (
        P(None, ("elem", "clus")),
        P(None, None, ("elem", "clus")),
        P(),
        P(),
        P(("elem", "clus")),
        P(("elem", "clus")),
        P(("elem", "clus")),
        P(None, ("elem", "clus")),
    )
    return jax.shard_map(
        functools.partial(on_device, mesh.shape["elem"]),
        mesh=mesh,
        in_specs=in_specs,
        out_specs=P(None, ("elem", "clus")),
        check_vma=False,
    )
```

time: 235 us -> 34 us (0.14)
  matrix products: 81.1 us -> 0 us
  starting transfers between devices: 46.8 us -> 0 us
  other arithmetic: 42.8 us -> 0.7 us
  local copies, waits for them, and re-layouts: 44.5 us -> 3.68 us
  Pallas kernels: 0 us -> 29.2 us
  blocking collectives: 12.5 us -> 0 us
  waiting for transfers between devices: 5.97 us -> 0 us
    dot_general x10 -> x0, matrix products: 81.1 us -> none  [the longest x1 20.6 us: project_traces(): jnp.einsum('xaf,abf->xbf', left_map, traces, precision=highest)]
    scatter-add x8 -> x0, other arithmetic: 41.1 us -> none  [the longest x1 14.7 us: coarse_correction(): counts = jnp.zeros((2 * NV_DEV,), jnp.float32).at[flat_ids].add(jnp.ones(...]
    pallas_call x0 -> x1, Pallas kernels: none -> 29.2 us  [on_device(): pl.pallas_call(functools.partial(kernel, n_elem), out_shape=jax.ShapeDtyp...]
    ppermute x6 -> x0, starting transfers between devices: 25.7 us -> none  [the longest x3 20 us: extended(): after = lax.ppermute(initial, axis, down)]
    all_to_all x2 -> x0, starting transfers between devices: 21.1 us -> none  [group_swap(): lax.all_to_all(columns, 'clus', split_axis=1, concat_axis=1, tiled=True)]
    gather x4 -> x0, local copies, waits for them, and re-layouts: 17.2 us -> none  [the longest x1 13.2 us: coarse_correction(): return coarse[window_ids]]
    psum x1 -> x0, blocking collectives: 12.5 us -> none  [coarse_correction(): totals, counts = lax.psum((totals, counts), 'clus')]
    transpose x2 -> x0, local copies, waits for them, and re-layouts: 8.84 us -> none  [the longest x1 4.44 us: project_traces(): jnp.einsum('ybf,xbf->xyf', right_map, partial_rows, precision=highest)]
  transfers between devices with their start and end apart: 8 -> 0, of which waited for: 2 -> 0; matrix products, arithmetic and copies ran while one was open for 21% -> 0% of each run, Pallas kernels for 0% -> 0%
where the time goes in v1:
time: 34 us; the launch traced here: 33.7 us
  Pallas kernels  29.2 us (86%)
  local copies, waits for them, and re-layouts  3.68 us (11%)
  other arithmetic  0.7 us (2%)
    pallas_call x1, Pallas kernels, on_device(): pl.pallas_call(functools.partial(kernel, n_elem), out_shape=jax.ShapeDtyp...  29.2 us
    unnamed x16, local copies, waits for them, and re-layouts  2.62 us
    broadcast_in_dim x1, local copies, waits for them, and re-layouts, on_device(): mats = jnp.concatenate([interp, derivative[None]], axis=0)  0.81 us
    transpose x1, other arithmetic, on_device(): mats.transpose(0, 2, 1)  0.69 us

profile of v1, /device:TPU:1, one launch (start us, length us, event | category | flops | bytes accessed | tf_op | source)
XLA Modules:
  0.0 33.7 jit_solution(7368288040245803588)
XLA Ops:
  0.0 0.0 copy-start.6
  0.0 0.0 copy-start.1
  0.0 0.8 %copy.12 = f32[1,8,8]{1,2,0:T(8,128)S(1)} copy(f32[1,8,8]{2,1,0:T(8,128)} %bitcast.15) | data formatting | bytes 512 | tf_op jit(solution)/shard_map/broadcast_in_dim | solution.py:385
  0.8 0.0 copy-done.6
  0.8 0.1 copy.11
  0.9 0.7 %maximum_bitcast_fusion = f32[3,8,8]{1,2,0:T(8,128)S(1)} fusion(f32[1,8,8]{2,1,0:T(8,128)} %bitcast.16, f32[2,8,8]{2,1,0:T(8,128)S(1)} %copy-done.6), kind=kLoop, calls=%fused_computation.1 | loop fusion | flops 192 | bytes 1536 | tf_op jit(solution)/shard_map/transpose | solution.py:386
  1.6 0.1 broadcast_in_dim.16
  1.7 0.1 copy.15.mb_hbm
  1.8 0.0 copy-start.2
  1.8 0.0 copy-start.3
  1.8 0.0 copy-start.4
  1.8 0.0 copy-start.5
  1.8 0.1 copy.14.ma_hbm
  1.9 0.0 copy-done.1
  1.9 0.6 %copy-done.2 = s32[1536]{0:T(1024)S(1)} copy-done((s32[1536]{0:T(1024)S(1)}, s32[1536]{0:T(1024)}, u32[]{:S(2)}) %copy-start.2) | copy-done | bytes 6168
  2.5 0.0 copy-done.3
  2.5 0.0 copy-done.4
  2.5 0.0 copy-done.5
  2.5 0.0 copy-start
  2.5 1.1 %copy-done = bf16[3,512,256]{2,1,0:T(8,128)(2,1)S(1)} copy-done((bf16[3,512,256]{2,1,0:T(8,128)(2,1)S(1)}, bf16[3,512,256]{2,1,0:T(8,128)(2,1)}, u32[]{:S(2)}) %copy-start) | copy-done | bytes 786456
  3.7 29.2 %shard_map.82 = f32[512,256]{1,0:T(8,128)S(1)} custom-call(f32[512,256]{1,0:T(8,128)S(1)} %copy-done.1, bf16[3,512,256]{2,1,0:T(8,128)(2,1)S(1)} %copy-done, f32[48,192]{1,0:T(8,128)S(1)} %copy.14.ma_hbm, f32[48,192]{1,0:T(8,128)S(1)} %copy.15.mb_hbm, s32[12,128]{1,0:T(8,128)S(1)} %bitcast.10, s32[12,128]{1,0:T(8,128)S(1)} %bitcast.11, ...), custom_call_target="tpu_custom_call" | custom-call | tf_op jit(solution)/shard_map/pallas_call | solution.py:391
  32.9 0.8 %copy.17 = f32[512,256]{1,0:T(8,128)} copy(f32[512,256]{1,0:T(8,128)S(1)} %shard_map.82) | data formatting | bytes 1048576
  (4 shorter events, 0.0 us)
Async XLA Ops:
  0.0 0.8 %copy-start.6 = (f32[2,8,8]{2,1,0:T(8,128)S(1)}, f32[2,8,8]{2,1,0:T(8,128)}, u32[]{:S(2)}) copy-start(f32[2,8,8]{2,1,0:T(8,128)} %param.11) | copy-start | bytes 1540
  0.0 1.9 %copy-start.1 = (f32[512,256]{1,0:T(8,128)S(1)}, f32[512,256]{1,0:T(8,128)}, u32[]{:S(2)}) copy-start(f32[512,256]{1,0:T(8,128)} %u_hbm.1) | copy-start | bytes 1572868
  1.8 0.7 %copy-start.2 = (s32[1536]{0:T(1024)S(1)}, s32[1536]{0:T(1024)}, u32[]{:S(2)}) copy-start(s32[1536]{0:T(1024)} %param.12) | copy-start | bytes 18436
  1.8 0.7 %copy-start.3 = (s32[1536]{0:T(1024)S(1)}, s32[1536]{0:T(1024)}, u32[]{:S(2)}) copy-start(s32[1536]{0:T(1024)} %param.13) | copy-start | bytes 18436
  1.8 0.7 %copy-start.4 = (s32[8,256]{1,0:T(8,128)S(1)}, s32[8,256]{1,0:T(8,128)}, u32[]{:S(2)}) copy-start(s32[8,256]{1,0:T(8,128)} %vid_hbm.1) | copy-start | bytes 24580
  1.8 0.7 %copy-start.5 = (s32[384]{0:T(512)S(1)}, s32[384]{0:T(512)}, u32[]{:S(2)}) copy-start(s32[384]{0:T(512)} %param.14) | copy-start | bytes 4612
  2.5 1.1 %copy-start = (bf16[3,512,256]{2,1,0:T(8,128)(2,1)S(1)}, bf16[3,512,256]{2,1,0:T(8,128)(2,1)}, u32[]{:S(2)}) copy-start(bf16[3,512,256]{2,1,0:T(8,128)(2,1)} %met_hbm.1) | copy-start | bytes 2359300

commit v2 on v1

--- a/solution.py
+++ b/solution.py
@@ -57,8 +57,8 @@
     n_elem,
     u_hbm,
     met_hbm,
-    ma_hbm,
-    mb_hbm,
+    deriv_hbm,
+    interp_hbm,
     lvl_hbm,
     tgt_hbm,
     slot_hbm,
@@ -66,6 +66,9 @@
     out,
     u,
     met,
+    deriv,
+    interp,
+    small,
     ma,
     mb,
     lvl,
@@ -103,6 +106,13 @@
     nxt = lax.rem(e + 1, n_elem)
     prv = lax.rem(e + n_elem - 1, n_elem)
 
+    barrier = pltpu.get_barrier_semaphore()
+    for peer in (nxt, prv):
+        pl.semaphore_signal(barrier, inc=1, device_id={"elem": peer}, device_id_type=MESH)
+    for k in range(1, GROUP):
+        peer = lax.rem(c + k, GROUP)
+        pl.semaphore_signal(barrier, inc=1, device_id={"clus": peer}, device_id_type=MESH)
+
     loads = [
         pltpu.make_async_copy(src, dst, in_sem.at[n])
         for n, (src, dst) in enumerate(
@@ -110,8 +120,8 @@
                 (tgt_hbm, tgt),
                 (u_hbm.at[:, 0:128], u.at[0]),
                 (u_hbm.at[:, 128:256], u.at[1]),
-                (ma_hbm, ma),
-                (mb_hbm, mb),
+                (interp_hbm, interp),
+                (deriv_hbm, deriv),
                 (lvl_hbm, lvl),
                 (vid_hbm, vid),
                 (slot_hbm, slot),
@@ -129,21 +139,31 @@
         for side in range(2):
             acc[side, place, :] = acc[side, place, :] + value[:, 128 * side : 128 * side + 128]
 
-    barrier = pltpu.get_barrier_semaphore()
-    for peer in (nxt, prv):
-        pl.semaphore_signal(barrier, inc=1, device_id={"elem": peer}, device_id_type=MESH)
-    for k in range(1, GROUP):
-        peer = lax.rem(c + k, GROUP)
-        pl.semaphore_signal(barrier, inc=1, device_id={"clus": peer}, device_id_type=MESH)
-
+    def fill_pick(first, last):
+        rows = iota((last - first, 128), 0) + first
+        for b in range(FACES // 128):
+            hot = jnp.where(rows == tgt[b : b + 1, :], 1.0, 0.0).astype(BF16)
+            pick[first:last, b * 128 : (b + 1) * 128] = hot
+
+    small[...] = jnp.zeros_like(small)
     loads[0].wait()
-    rows = iota((COLS, 128), 0)
-    for b in range(FACES // 128):
-        hot = jnp.where(rows == tgt[b : b + 1, :], 1.0, 0.0).astype(BF16)
-        pick[:, b * 128 : (b + 1) * 128] = hot
+    fill_pick(M_DEV, COLS)
 
     loads[3].wait()
     loads[4].wait()
+    small[0:8, 0:8] = interp[0]
+    small[8:16, 0:8] = interp[1]
+    small[16:24, 0:8] = deriv[...]
+    lane = iota((128, 384), 1)
+    inner = jnp.where(lane < 192, (lane & 63) >> 3, lane & 7)
+
+    def widened(x, which):
+        spread = jnp.where(iota((128, 384), 0) == inner + 8 * which, 1.0, 0.0)
+        return jnp.dot(x, spread, precision=lax.Precision.HIGHEST, preferred_element_type=F32)
+
+    wide = widened(small[0:24, :], 0)
+    ma[0:24, :] = wide[:, 0:192]
+    mb[0:24, :] = wide[:, 192:384]
 
     def kron(first, second):
         return jnp.concatenate(
@@ -269,12 +289,49 @@
     mine = pl.ds(pl.multiple_of(c * CAP_C, CAP_C), CAP_C)
     recv_g[mine, :] = send_g[mine, :]
 
+    fill_pick(0, M_DEV)
     own[...] = halves(mm(proj[...], pick[0:M_DEV, :], NT))
     loads[7].wait()
     rows2 = iota((M_DEV, 128), 0)
     for b in range(SLOTS // 128):
         hot = jnp.where(rows2 == slot[b : b + 1, :], 1.0, 0.0).astype(BF16)
         pick2[:, b * 128 : (b + 1) * 128] = hot
+
+    turned_small = small[...].T[0:8]
+    for which in range(3):
+        wide = widened(turned_small, which)
+        ma[24 + 8 * which : 32 + 8 * which, :] = wide[:, 0:192]
+        mb[24 + 8 * which : 32 + 8 * which, :] = wide[:, 192:384]
+    backward = three_terms(jnp.concatenate([kron(r + 3, s + 3) for r, s in pairs], axis=0))
+
+    for copy in first_round:
+        copy.wait()
+    group_in = recv_g[...]
+    arrived = jnp.concatenate([recv_e[0], recv_e[1], group_in.T[0:64]], axis=1)
+    hi, lo = split(arrived)
+    mortar = own[...] + halves(mm(jnp.concatenate([hi, lo], axis=0), pick2[...], NT))
+    hi, lo = split(mortar)
+    mortar2 = jnp.concatenate([hi, lo], axis=0)
+    answers = halves(mm(mortar2, pick2[...]))
+    coarse_sum = group_in[0:16]
+    for i in range(1, GROUP):
+        coarse_sum = coarse_sum + group_in[16 * i : 16 * i + 16]
+    send_e2[0, 0:64, :] = answers[:, 0:128]
+    send_e2[1, 0:64, :] = answers[:, 128:256]
+    send_e2[0, 64:80, :] = coarse_sum
+    send_e2[1, 64:80, :] = coarse_sum
+    shifted = pltpu.roll(answers[:, 256:384], 120, 1)
+    turned = jnp.concatenate([answers[:, 256:384], shifted], axis=0).T
+    for i in range(GROUP):
+        send_g2[8 * i : 8 * i + 8, :] = turned[16 * i : 16 * i + 8, :]
+    second_round = edge_copies(send_e2, recv_e2, se2_sem, re2_sem)
+    second_round += group_copies(send_g2, recv_g2, sg2_sem, rg2_sem, CAP_C // 2)
+    for copy in second_round:
+        copy.start()
+    mine2 = pl.ds(pl.multiple_of(c * 8, 8), 8)
+    recv_g2[mine2, :] = send_g2[mine2, :]
+
+    picked[...] = halves(mm(mortar2, pick[0:M_DEV, :]))
 
     loads[8].wait()
     d_first = first_kron(2)
@@ -306,36 +363,15 @@
         back = mm(t_first, stacked(part))
         for i in range(8):
             add_rows(slice(64 * i + 8 * j, 64 * i + 8 * j + 8), back[8 * i : 8 * i + 8])
-    backward = three_terms(jnp.concatenate([kron(r + 3, s + 3) for r, s in pairs], axis=0))
-
-    for copy in first_round:
-        copy.wait()
-    group_in = recv_g[...]
-    arrived = jnp.concatenate([recv_e[0], recv_e[1], group_in.T[0:64]], axis=1)
-    hi, lo = split(arrived)
-    mortar = own[...] + halves(mm(jnp.concatenate([hi, lo], axis=0), pick2[...], NT))
-    hi, lo = split(mortar)
-    mortar2 = jnp.concatenate([hi, lo], axis=0)
-    answers = halves(mm(mortar2, pick2[...]))
-    coarse_sum = group_in[0:16]
-    for i in range(1, GROUP):
-        coarse_sum = coarse_sum + group_in[16 * i : 16 * i + 16]
-    send_e2[0, 0:64, :] = answers[:, 0:128]
-    send_e2[1, 0:64, :] = answers[:, 128:256]
-    send_e2[0, 64:80, :] = coarse_sum
-    send_e2[1, 64:80, :] = coarse_sum
-    send_g2[...] = jnp.concatenate([answers[:, 256:384], jnp.zeros((64, 128), F32)], axis=0).T
-    second_round = edge_copies(send_e2, recv_e2, se2_sem, re2_sem)
-    second_round += group_copies(send_g2, recv_g2, sg2_sem, rg2_sem, CAP_C)
-    for copy in second_round:
-        copy.start()
-    recv_g2[mine, :] = send_g2[mine, :]
-
-    picked[...] = halves(mm(mortar2, pick[0:M_DEV, :]))
 
     for copy in second_round:
         copy.wait()
-    returned = jnp.concatenate([recv_e2[0, 0:64, :], recv_e2[1, 0:64, :], recv_g2[...].T[0:64]], axis=1)
+    turned = jnp.concatenate(
+        [recv_g2[8 * (i // 2) : 8 * (i // 2) + 8, :] for i in range(2 * GROUP)], axis=0
+    ).T
+    odd = (iota((64, 128), 1) & 8) != 0
+    from_group = jnp.where(odd, turned[64:128], turned[0:64])
+    returned = jnp.concatenate([recv_e2[0, 0:64, :], recv_e2[1, 0:64, :], from_group], axis=1)
     hi, lo = split(returned)
     returned2 = jnp.concatenate([hi, lo], axis=0)
     before = recv_e2[0, 64:80, :]
@@ -382,11 +418,7 @@
 
 
 def on_device(n_elem, nodal, metric, derivative, interp, face_level, face_target, slot_mortar, vertex_ids):
-    mats = jnp.concatenate([interp, derivative[None]], axis=0)
-    mats = jnp.concatenate([mats, mats.transpose(0, 2, 1)], axis=0).reshape(48, 8)
-    first = jnp.broadcast_to(mats[:, None, :, None], (48, 3, 8, 8)).reshape(48, 192)
-    second = jnp.broadcast_to(mats[:, None, None, :], (48, 3, 8, 8)).reshape(48, 192)
-    anywhere = pl.BlockSpec(memory_space=pl.ANY)
+    anywhere = pl.BlockSpec(memory_space=pltpu.HBM)
     dma = pltpu.SemaphoreType.DMA
     return pl.pallas_call(
         functools.partial(kernel, n_elem),
@@ -396,6 +428,9 @@
         scratch_shapes=[
             pltpu.VMEM((2, NODES, 128), F32),
             pltpu.VMEM((3, NODES, E_DEV), BF16),
+            pltpu.VMEM((8, 8), F32),
+            pltpu.VMEM((2, 8, 8), F32),
+            pltpu.VMEM((128, 128), F32),
             pltpu.VMEM((48, 192), F32),
             pltpu.VMEM((48, 192), F32),
             pltpu.VMEM((12, 128), jnp.int32),
@@ -415,9 +450,9 @@
             pltpu.VMEM((2, 64, 128), F32),
             pltpu.VMEM((128, 128), F32),
             pltpu.VMEM((2, 80, 128), F32),
-            pltpu.VMEM((128, 128), F32),
+            pltpu.VMEM((64, 128), F32),
             pltpu.VMEM((2, 80, 128), F32),
-            pltpu.VMEM((128, 128), F32),
+            pltpu.VMEM((64, 128), F32),
             dma((9,)),
             dma((2,)),
             dma((2,)),
@@ -432,14 +467,19 @@
             collective_id=0, has_side_effects=True, vmem_limit_bytes=48 * 1024 * 1024
         ),
     )(
-        nodal,
-        metric,
-        first,
-        second,
-        face_level.reshape(12, 128),
-        face_target.reshape(12, 128),
-        slot_mortar.reshape(3, 128),
-        vertex_ids,
+        *[
+            pltpu.with_memory_space_constraint(x, pltpu.HBM)
+            for x in (
+                nodal,
+                metric,
+                derivative,
+                interp,
+                face_level.reshape(12, 128),
+                face_target.reshape(12, 128),
+                slot_mortar.reshape(3, 128),
+                vertex_ids,
+            )
+        ]
     )
 
 

time: 34 us -> 30.4 us (0.89)
  local copies, waits for them, and re-layouts: 3.68 us -> 0.8 us
  other arithmetic: 0.7 us -> 0 us
    unnamed x16 -> x1, local copies, waits for them, and re-layouts: 2.62 us -> 0.8 us
    broadcast_in_dim x4 -> x0, local copies, waits for them, and re-layouts: 0.91 us -> none  [the longest x1 0.81 us: on_device(): mats = jnp.concatenate([interp, derivative[None]], axis=0)]
    transpose x1 -> x0, other arithmetic: 0.69 us -> none  [on_device(): mats.transpose(0, 2, 1)]
where the time goes in v2:
time: 30.4 us; the launch traced here: 30.3 us
  Pallas kernels  29.5 us (97%)
  local copies, waits for them, and re-layouts  0.8 us (3%)
    pallas_call x1, Pallas kernels, on_device(): pl.pallas_call(functools.partial(kernel, n_elem), out_shape=jax.ShapeDtyp...  29.5 us
    unnamed x1, local copies, waits for them, and re-layouts  0.8 us

profile of v2, /device:TPU:1, one launch (start us, length us, event | category | flops | bytes accessed | tf_op | source)
XLA Modules:
  0.0 30.3 jit_solution(13612560413611757156)
XLA Ops:
  0.0 29.5 %shard_map.82 = f32[512,256]{1,0:T(8,128)S(1)} custom-call(f32[512,256]{1,0:T(8,128)} %u_hbm.1, bf16[3,512,256]{2,1,0:T(8,128)(2,1)} %met_hbm.1, f32[8,8]{1,0:T(8,128)} %deriv_hbm.1, f32[2,8,8]{2,1,0:T(8,128)} %interp_hbm.1, s32[12,128]{1,0:T(8,128)} %bitcast.3, s32[12,128]{1,0:T(8,128)} %bitcast.4, s32[3,128]{1,0:T(4,128)} %bitcast.5, s32[8,256]{1,0:T(8,128)} %vid_hbm.1), custom_call_target="tpu_custom_call" | custom-call | tf_op jit(solution)/shard_map/pallas_call | solution.py:423
  29.5 0.8 %copy.10 = f32[512,256]{1,0:T(8,128)} copy(f32[512,256]{1,0:T(8,128)S(1)} %shard_map.82) | data formatting | bytes 1048576

commit v3 on v2

--- a/solution.py
+++ b/solution.py
@@ -13,6 +13,7 @@
 M_DEV = 512
 SLOTS = 2 * CAP_E + GROUP * CAP_C
 COLS = M_DEV + SLOTS
+GROUP_COL = M_DEV + 2 * CAP_E
 NV_DEV = 256
 E_DEV = 256
 FACES = 6 * E_DEV
@@ -41,6 +42,11 @@
 
 def halves(x):
     return x[:64] + x[64:]
+
+
+def two_terms(x):
+    hi, lo = split(x)
+    return jnp.concatenate([hi, lo], axis=0)
 
 
 def iota(shape, axis):
@@ -80,7 +86,10 @@
     corner_hot,
     proj,
     own,
-    picked,
+    faces,
+    answers,
+    arrived,
+    same,
     grad0,
     acc,
     send_e,
@@ -106,13 +115,6 @@
     nxt = lax.rem(e + 1, n_elem)
     prv = lax.rem(e + n_elem - 1, n_elem)
 
-    barrier = pltpu.get_barrier_semaphore()
-    for peer in (nxt, prv):
-        pl.semaphore_signal(barrier, inc=1, device_id={"elem": peer}, device_id_type=MESH)
-    for k in range(1, GROUP):
-        peer = lax.rem(c + k, GROUP)
-        pl.semaphore_signal(barrier, inc=1, device_id={"clus": peer}, device_id_type=MESH)
-
     loads = [
         pltpu.make_async_copy(src, dst, in_sem.at[n])
         for n, (src, dst) in enumerate(
@@ -129,8 +131,15 @@
             ]
         )
     ]
-    for load in loads:
+    for load in loads[:8]:
         load.start()
+
+    barrier = pltpu.get_barrier_semaphore()
+    for peer in (nxt, prv):
+        pl.semaphore_signal(barrier, inc=1, device_id={"elem": peer}, device_id_type=MESH)
+    for k in range(1, GROUP):
+        peer = lax.rem(c + k, GROUP)
+        pl.semaphore_signal(barrier, inc=1, device_id={"clus": peer}, device_id_type=MESH)
 
     def node_rows(ref, place):
         return jnp.concatenate([ref[0, place, :], ref[1, place, :]], axis=1)
@@ -196,30 +205,34 @@
 
     loads[1].wait()
     loads[2].wait()
+    loads[8].start()
     loads[5].wait()
-    for f in range(6):
-        if f == 0:
-            trace = node_rows(u, slice(0, 64))
-        elif f == 1:
-            trace = node_rows(u, slice(448, 512))
-        elif f == 2:
-            trace = jnp.concatenate([node_rows(u, slice(64 * i, 64 * i + 8)) for i in range(8)], axis=0)
-        elif f == 3:
-            trace = jnp.concatenate(
-                [node_rows(u, slice(64 * i + 56, 64 * i + 64)) for i in range(8)], axis=0
-            )
-        else:
-            first = 0 if f == 4 else 7
-            trace = node_rows(u, pl.ds(first, 64, stride=8))
-        level = jnp.concatenate([lvl[2 * f : 2 * f + 1, :], lvl[2 * f + 1 : 2 * f + 2, :]], axis=1)
-        level = jnp.broadcast_to(level, (64, E_DEV))
-        every = mm(forth, stacked(trace))
-        chosen = trace
+    def across(ref, first, count):
+        row = jnp.concatenate([ref[n : n + 1, :] for n in range(first, first + count)], axis=1)
+        return jnp.broadcast_to(row, (64, 128 * count))
+
+    def by_level(level, mats, value):
+        every = mm(mats, stacked(value))
+        chosen = value
         for n in range(4):
             chosen = jnp.where(level == n + 1, every[64 * n : 64 * n + 64], chosen)
-        hi, lo = split(chosen)
-        proj[0:64, f * 256 : (f + 1) * 256] = hi
-        proj[64:128, f * 256 : (f + 1) * 256] = lo
+        return chosen
+
+    far = [slice(8 * j, 8 * j + 8) for j in range(64)]
+    trace = jnp.concatenate(
+        [
+            node_rows(u, slice(0, 64)),
+            node_rows(u, slice(448, 512)),
+            jnp.concatenate([node_rows(u, far[8 * i]) for i in range(8)], axis=0),
+            jnp.concatenate([node_rows(u, far[8 * i + 7]) for i in range(8)], axis=0),
+            node_rows(u, pl.ds(0, 64, stride=8)),
+            node_rows(u, pl.ds(7, 64, stride=8)),
+        ],
+        axis=1,
+    )
+    hi, lo = split(by_level(across(lvl, 0, 12), forth, trace))
+    proj[0:64, :] = hi
+    proj[64:128, :] = lo
 
     loads[6].wait()
     away = vid[...] - e * NV_DEV
@@ -246,10 +259,8 @@
         sums = sums + mm(jnp.concatenate(parts, axis=0).astype(BF16), hot, NT)
     local = jnp.concatenate([sums[0:8] + sums[8:16], sums[16:24]], axis=0)
 
-    leaving = halves(mm(proj[...], pick[M_DEV:COLS, :], NT))
-    send_e[0] = leaving[:, 0:128]
-    send_e[1] = leaving[:, 128:256]
-    turned = jnp.concatenate([leaving[:, 256:384], jnp.zeros((64, 128), F32)], axis=0).T
+    leaving = halves(mm(proj[...], pick[GROUP_COL:COLS, :], NT))
+    turned = jnp.concatenate([leaving, jnp.zeros((64, 128), F32)], axis=0).T
     send_g[...] = turned + jnp.concatenate([local] * GROUP, axis=0)
 
     def edge_copies(src, dst, ssem, rsem):
@@ -282,9 +293,14 @@
         return copies
 
     pl.semaphore_wait(barrier, GROUP + 1)
-    first_round = edge_copies(send_e, recv_e, se_sem, re_sem)
-    first_round += group_copies(send_g, recv_g, sg_sem, rg_sem, CAP_C)
-    for copy in first_round:
+    group_round = group_copies(send_g, recv_g, sg_sem, rg_sem, CAP_C)
+    for copy in group_round:
+        copy.start()
+    leaving = halves(mm(proj[...], pick[M_DEV:GROUP_COL, :], NT))
+    send_e[0] = leaving[:, 0:128]
+    send_e[1] = leaving[:, 128:256]
+    edge_round = edge_copies(send_e, recv_e, se_sem, re_sem)
+    for copy in edge_round:
         copy.start()
     mine = pl.ds(pl.multiple_of(c * CAP_C, CAP_C), CAP_C)
     recv_g[mine, :] = send_g[mine, :]
@@ -304,34 +320,48 @@
         mb[24 + 8 * which : 32 + 8 * which, :] = wide[:, 192:384]
     backward = three_terms(jnp.concatenate([kron(r + 3, s + 3) for r, s in pairs], axis=0))
 
-    for copy in first_round:
+    level_row = jnp.concatenate([lvl[n : n + 1, :] for n in range(12)], axis=1)
+    level_row = jnp.broadcast_to(level_row, (16, FACES)).astype(F32).astype(BF16)
+    slot_level = mm(level_row, pick[M_DEV:COLS, :], NT)[0:1]
+    slot_level = jnp.broadcast_to(slot_level, (64, SLOTS))
+
+    slot_row = jnp.concatenate([slot[b : b + 1, :] for b in range(3)], axis=1)
+    for b in range(3):
+        column = jnp.broadcast_to(slot[b : b + 1, :], (128, 128)).T
+        column = jnp.concatenate([column] * 3, axis=1)
+        same[128 * b : 128 * b + 128, :] = jnp.where(column == slot_row, 1.0, 0.0).astype(BF16)
+
+    answers[...] = halves(mm(two_terms(own[...]), pick2[...]))
+    for copy in edge_round:
+        copy.wait()
+    arrived[:, 0:256] = two_terms(jnp.concatenate([recv_e[0], recv_e[1]], axis=1))
+    answers[...] = answers[...] + halves(mm(arrived[:, 0:256], same[0:256, :]))
+    for copy in group_round:
         copy.wait()
     group_in = recv_g[...]
-    arrived = jnp.concatenate([recv_e[0], recv_e[1], group_in.T[0:64]], axis=1)
-    hi, lo = split(arrived)
-    mortar = own[...] + halves(mm(jnp.concatenate([hi, lo], axis=0), pick2[...], NT))
-    hi, lo = split(mortar)
-    mortar2 = jnp.concatenate([hi, lo], axis=0)
-    answers = halves(mm(mortar2, pick2[...]))
+    from_group = two_terms(group_in.T[0:64])
+    arrived[:, 256:384] = from_group
+    answer = answers[:, 256:384] + halves(mm(from_group, same[256:384, 256:384]))
+    shifted = pltpu.roll(answer, 120, 1)
+    turned = jnp.concatenate([answer, shifted], axis=0).T
+    for i in range(GROUP):
+        send_g2[8 * i : 8 * i + 8, :] = turned[16 * i : 16 * i + 8, :]
+    group_round = group_copies(send_g2, recv_g2, sg2_sem, rg2_sem, CAP_C // 2)
+    for copy in group_round:
+        copy.start()
+    answer = answers[:, 0:256] + halves(mm(from_group, same[256:384, 0:256]))
     coarse_sum = group_in[0:16]
     for i in range(1, GROUP):
         coarse_sum = coarse_sum + group_in[16 * i : 16 * i + 16]
-    send_e2[0, 0:64, :] = answers[:, 0:128]
-    send_e2[1, 0:64, :] = answers[:, 128:256]
+    send_e2[0, 0:64, :] = answer[:, 0:128]
+    send_e2[1, 0:64, :] = answer[:, 128:256]
     send_e2[0, 64:80, :] = coarse_sum
     send_e2[1, 64:80, :] = coarse_sum
-    shifted = pltpu.roll(answers[:, 256:384], 120, 1)
-    turned = jnp.concatenate([answers[:, 256:384], shifted], axis=0).T
-    for i in range(GROUP):
-        send_g2[8 * i : 8 * i + 8, :] = turned[16 * i : 16 * i + 8, :]
-    second_round = edge_copies(send_e2, recv_e2, se2_sem, re2_sem)
-    second_round += group_copies(send_g2, recv_g2, sg2_sem, rg2_sem, CAP_C // 2)
-    for copy in second_round:
+    edge_round = edge_copies(send_e2, recv_e2, se2_sem, re2_sem)
+    for copy in edge_round:
         copy.start()
     mine2 = pl.ds(pl.multiple_of(c * 8, 8), 8)
     recv_g2[mine2, :] = send_g2[mine2, :]
-
-    picked[...] = halves(mm(mortar2, pick[0:M_DEV, :]))
 
     loads[8].wait()
     d_first = first_kron(2)
@@ -364,16 +394,15 @@
         for i in range(8):
             add_rows(slice(64 * i + 8 * j, 64 * i + 8 * j + 8), back[8 * i : 8 * i + 8])
 
-    for copy in second_round:
+    mortar = own[...] + halves(mm(arrived[...], pick2[...], NT))
+    picked = halves(mm(two_terms(mortar), pick[0:M_DEV, :]))
+    faces[...] = by_level(across(lvl, 0, 12), backward, picked)
+
+    for copy in edge_round:
         copy.wait()
-    turned = jnp.concatenate(
-        [recv_g2[8 * (i // 2) : 8 * (i // 2) + 8, :] for i in range(2 * GROUP)], axis=0
-    ).T
-    odd = (iota((64, 128), 1) & 8) != 0
-    from_group = jnp.where(odd, turned[64:128], turned[0:64])
-    returned = jnp.concatenate([recv_e2[0, 0:64, :], recv_e2[1, 0:64, :], from_group], axis=1)
-    hi, lo = split(returned)
-    returned2 = jnp.concatenate([hi, lo], axis=0)
+    value = jnp.concatenate([recv_e2[0, 0:64, :], recv_e2[1, 0:64, :]], axis=1)
+    value = two_terms(by_level(slot_level[:, 0:256], backward, value))
+    faces[...] = faces[...] + halves(mm(value, pick[M_DEV:GROUP_COL, :]))
     before = recv_e2[0, 64:80, :]
     after = recv_e2[1, 64:80, :]
 
@@ -391,30 +420,31 @@
     spread = mm(coarse2, corner_hot[...])
     spread = spread[0:8] + spread[8:16]
 
-    for f in range(6):
-        span = slice(f * 256, (f + 1) * 256)
-        value = picked[:, span] + halves(mm(returned2, pick[M_DEV:COLS, span]))
-        level = jnp.concatenate([lvl[2 * f : 2 * f + 1, :], lvl[2 * f + 1 : 2 * f + 2, :]], axis=1)
-        level = jnp.broadcast_to(level, (64, E_DEV))
-        every = mm(backward, stacked(value))
-        chosen = value
-        for n in range(4):
-            chosen = jnp.where(level == n + 1, every[64 * n : 64 * n + 64], chosen)
-        if f < 2:
-            add_rows(slice(448 * f, 448 * f + 64), chosen)
-        elif f < 4:
-            for i in range(8):
-                first = 64 * i + 56 * (f - 2)
-                add_rows(slice(first, first + 8), chosen[8 * i : 8 * i + 8])
-        else:
-            add_rows(pl.ds(7 * (f - 4), 64, stride=8), chosen)
     for corner in range(8):
         row = 7 * (64 * (corner // 4) + 8 * (corner // 2 % 2) + corner % 2)
         here = eight == high[corner : corner + 1, :]
         fix = jnp.where(here, spread[:, corner * 256 : (corner + 1) * 256], 0.0)
         add_rows(slice(row, row + 1), jnp.sum(fix, axis=0, keepdims=True))
-    out[:, 0:128] = acc[0]
-    out[:, 128:256] = acc[1]
+    for copy in group_round:
+        copy.wait()
+    turned = jnp.concatenate(
+        [recv_g2[8 * (i // 2) : 8 * (i // 2) + 8, :] for i in range(2 * GROUP)], axis=0
+    ).T
+    odd = (iota((64, 128), 1) & 8) != 0
+    value = jnp.where(odd, turned[64:128], turned[0:64])
+    value = two_terms(by_level(slot_level[:, 256:384], backward, value))
+    total = faces[...] + halves(mm(value, pick[GROUP_COL:COLS, :]))
+    add_rows(pl.ds(0, 64, stride=8), total[:, 1024:1280])
+    add_rows(pl.ds(7, 64, stride=8), total[:, 1280:1536])
+    for i in range(8):
+        block = node_rows(acc, slice(64 * i, 64 * i + 64))
+        if i == 0:
+            block = block + total[:, 0:256]
+        if i == 7:
+            block = block + total[:, 256:512]
+        near = block[0:8] + total[8 * i : 8 * i + 8, 512:768]
+        away = block[56:64] + total[8 * i : 8 * i + 8, 768:1024]
+        out[64 * i : 64 * i + 64, :] = jnp.concatenate([near, block[8:56], away], axis=0)
 
 
 def on_device(n_elem, nodal, metric, derivative, interp, face_level, face_target, slot_mortar, vertex_ids):
@@ -443,6 +473,9 @@
             pltpu.VMEM((128, FACES), BF16),
             pltpu.VMEM((64, M_DEV), F32),
             pltpu.VMEM((64, FACES), F32),
+            pltpu.VMEM((64, SLOTS), F32),
+            pltpu.VMEM((128, SLOTS), BF16),
+            pltpu.VMEM((SLOTS, SLOTS), BF16),
             pltpu.VMEM((NODES, E_DEV), F32),
             pltpu.VMEM((2, NODES, 128), F32),
             pltpu.VMEM((2, 64, 128), F32),

time: 30.4 us -> 29.3 us (0.964)
  Pallas kernels: 29.5 us -> 28.3 us
    pallas_call x1, Pallas kernels: 29.5 us -> 28.3 us  [on_device(): pl.pallas_call(functools.partial(kernel, n_elem), out_shape=jax.ShapeDtyp...]
where the time goes in v3:
time: 29.3 us; the launch traced here: 29.1 us
  Pallas kernels  28.3 us (97%)
  local copies, waits for them, and re-layouts  0.8 us (3%)
    pallas_call x1, Pallas kernels, on_device(): pl.pallas_call(functools.partial(kernel, n_elem), out_shape=jax.ShapeDtyp...  28.3 us
    unnamed x1, local copies, waits for them, and re-layouts  0.8 us

profile of v3, /device:TPU:1, one launch (start us, length us, event | category | flops | bytes accessed | tf_op | source)
XLA Modules:
  0.0 29.1 jit_solution(16305106963310739990)
XLA Ops:
  0.0 28.3 %shard_map.82 = f32[512,256]{1,0:T(8,128)S(1)} custom-call(f32[512,256]{1,0:T(8,128)} %u_hbm.1, bf16[3,512,256]{2,1,0:T(8,128)(2,1)} %met_hbm.1, f32[8,8]{1,0:T(8,128)} %deriv_hbm.1, f32[2,8,8]{2,1,0:T(8,128)} %interp_hbm.1, s32[12,128]{1,0:T(8,128)} %bitcast.3, s32[12,128]{1,0:T(8,128)} %bitcast.4, s32[3,128]{1,0:T(4,128)} %bitcast.5, s32[8,256]{1,0:T(8,128)} %vid_hbm.1), custom_call_target="tpu_custom_call" | custom-call | tf_op jit(solution)/shard_map/pallas_call | solution.py:453
  28.3 0.8 %copy.10 = f32[512,256]{1,0:T(8,128)} copy(f32[512,256]{1,0:T(8,128)S(1)} %shard_map.82) | data formatting | bytes 1048576

commit v4 on v3

--- a/solution.py
+++ b/solution.py
@@ -100,6 +100,8 @@
     send_g2,
     recv_e2,
     recv_g2,
+    send_c,
+    recv_c,
     in_sem,
     se_sem,
     re_sem,
@@ -109,6 +111,8 @@
     re2_sem,
     sg2_sem,
     rg2_sem,
+    sc_sem,
+    rc_sem,
 ):
     e = lax.axis_index("elem")
     c = lax.axis_index("clus")
@@ -155,11 +159,11 @@
             pick[first:last, b * 128 : (b + 1) * 128] = hot
 
     small[...] = jnp.zeros_like(small)
-    loads[0].wait()
+    for load in loads[:7]:
+        load.wait()
+    loads[8].start()
     fill_pick(M_DEV, COLS)
 
-    loads[3].wait()
-    loads[4].wait()
     small[0:8, 0:8] = interp[0]
     small[8:16, 0:8] = interp[1]
     small[16:24, 0:8] = deriv[...]
@@ -203,10 +207,6 @@
     pairs = [(0, 0), (0, 1), (1, 0), (1, 1)]
     forth = three_terms(jnp.concatenate([kron(r, s) for r, s in pairs], axis=0))
 
-    loads[1].wait()
-    loads[2].wait()
-    loads[8].start()
-    loads[5].wait()
     def across(ref, first, count):
         row = jnp.concatenate([ref[n : n + 1, :] for n in range(first, first + count)], axis=1)
         return jnp.broadcast_to(row, (64, 128 * count))
@@ -234,7 +234,6 @@
     proj[0:64, :] = hi
     proj[64:128, :] = lo
 
-    loads[6].wait()
     away = vid[...] - e * NV_DEV
     total_vertices = n_elem * NV_DEV
     window = jnp.where(away < 0, away + total_vertices, away)
@@ -259,8 +258,10 @@
         sums = sums + mm(jnp.concatenate(parts, axis=0).astype(BF16), hot, NT)
     local = jnp.concatenate([sums[0:8] + sums[8:16], sums[16:24]], axis=0)
 
-    leaving = halves(mm(proj[...], pick[GROUP_COL:COLS, :], NT))
-    turned = jnp.concatenate([leaving, jnp.zeros((64, 128), F32)], axis=0).T
+    leaving = halves(mm(proj[...], pick[M_DEV:COLS, :], NT))
+    send_e[0] = leaving[:, 0:128]
+    send_e[1] = leaving[:, 128:256]
+    turned = jnp.concatenate([leaving[:, 256:384], jnp.zeros((64, 128), F32)], axis=0).T
     send_g[...] = turned + jnp.concatenate([local] * GROUP, axis=0)
 
     def edge_copies(src, dst, ssem, rsem):
@@ -278,7 +279,7 @@
 
     def group_copies(src, dst, ssem, rsem, rows):
         copies = []
-        for k in range(1, GROUP):
+        for k in (4, 5, 3, 2, 6, 7, 1):
             peer = lax.rem(c + k, GROUP)
             copies.append(
                 pltpu.make_async_remote_copy(
@@ -293,14 +294,9 @@
         return copies
 
     pl.semaphore_wait(barrier, GROUP + 1)
+    edge_round = edge_copies(send_e, recv_e, se_sem, re_sem)
     group_round = group_copies(send_g, recv_g, sg_sem, rg_sem, CAP_C)
-    for copy in group_round:
-        copy.start()
-    leaving = halves(mm(proj[...], pick[M_DEV:GROUP_COL, :], NT))
-    send_e[0] = leaving[:, 0:128]
-    send_e[1] = leaving[:, 128:256]
-    edge_round = edge_copies(send_e, recv_e, se_sem, re_sem)
-    for copy in edge_round:
+    for copy in edge_round + group_round:
         copy.start()
     mine = pl.ds(pl.multiple_of(c * CAP_C, CAP_C), CAP_C)
     recv_g[mine, :] = send_g[mine, :]
@@ -332,33 +328,36 @@
         same[128 * b : 128 * b + 128, :] = jnp.where(column == slot_row, 1.0, 0.0).astype(BF16)
 
     answers[...] = halves(mm(two_terms(own[...]), pick2[...]))
-    for copy in edge_round:
-        copy.wait()
-    arrived[:, 0:256] = two_terms(jnp.concatenate([recv_e[0], recv_e[1]], axis=1))
-    answers[...] = answers[...] + halves(mm(arrived[:, 0:256], same[0:256, :]))
     for copy in group_round:
         copy.wait()
     group_in = recv_g[...]
+    coarse_sum = group_in[0:16]
+    for i in range(1, GROUP):
+        coarse_sum = coarse_sum + group_in[16 * i : 16 * i + 16]
+    send_c[0] = coarse_sum
+    send_c[1] = coarse_sum
+    coarse_round = edge_copies(send_c, recv_c, sc_sem, rc_sem)
+    for copy in coarse_round:
+        copy.start()
     from_group = two_terms(group_in.T[0:64])
     arrived[:, 256:384] = from_group
-    answer = answers[:, 256:384] + halves(mm(from_group, same[256:384, 256:384]))
-    shifted = pltpu.roll(answer, 120, 1)
-    turned = jnp.concatenate([answer, shifted], axis=0).T
+    answers[...] = answers[...] + halves(mm(from_group, same[256:384, :]))
+    for copy in edge_round:
+        copy.wait()
+    from_edge = two_terms(jnp.concatenate([recv_e[0], recv_e[1]], axis=1))
+    arrived[:, 0:256] = from_edge
+    answer = answers[...] + halves(mm(from_edge, same[0:256, :]))
+    send_e2[0] = answer[:, 0:128]
+    send_e2[1] = answer[:, 128:256]
+    edge_round = edge_copies(send_e2, recv_e2, se2_sem, re2_sem)
+    for copy in edge_round:
+        copy.start()
+    shifted = pltpu.roll(answer[:, 256:384], 120, 1)
+    turned = jnp.concatenate([answer[:, 256:384], shifted], axis=0).T
     for i in range(GROUP):
         send_g2[8 * i : 8 * i + 8, :] = turned[16 * i : 16 * i + 8, :]
     group_round = group_copies(send_g2, recv_g2, sg2_sem, rg2_sem, CAP_C // 2)
     for copy in group_round:
-        copy.start()
-    answer = answers[:, 0:256] + halves(mm(from_group, same[256:384, 0:256]))
-    coarse_sum = group_in[0:16]
-    for i in range(1, GROUP):
-        coarse_sum = coarse_sum + group_in[16 * i : 16 * i + 16]
-    send_e2[0, 0:64, :] = answer[:, 0:128]
-    send_e2[1, 0:64, :] = answer[:, 128:256]
-    send_e2[0, 64:80, :] = coarse_sum
-    send_e2[1, 64:80, :] = coarse_sum
-    edge_round = edge_copies(send_e2, recv_e2, se2_sem, re2_sem)
-    for copy in edge_round:
         copy.start()
     mine2 = pl.ds(pl.multiple_of(c * 8, 8), 8)
     recv_g2[mine2, :] = send_g2[mine2, :]
@@ -398,13 +397,10 @@
     picked = halves(mm(two_terms(mortar), pick[0:M_DEV, :]))
     faces[...] = by_level(across(lvl, 0, 12), backward, picked)
 
-    for copy in edge_round:
+    for copy in coarse_round:
         copy.wait()
-    value = jnp.concatenate([recv_e2[0, 0:64, :], recv_e2[1, 0:64, :]], axis=1)
-    value = two_terms(by_level(slot_level[:, 0:256], backward, value))
-    faces[...] = faces[...] + halves(mm(value, pick[M_DEV:GROUP_COL, :]))
-    before = recv_e2[0, 64:80, :]
-    after = recv_e2[1, 64:80, :]
+    before = recv_c[0]
+    after = recv_c[1]
 
     def widen(mid, left, right):
         near = jnp.where(
@@ -433,7 +429,13 @@
     odd = (iota((64, 128), 1) & 8) != 0
     value = jnp.where(odd, turned[64:128], turned[0:64])
     value = two_terms(by_level(slot_level[:, 256:384], backward, value))
-    total = faces[...] + halves(mm(value, pick[GROUP_COL:COLS, :]))
+    faces[...] = faces[...] + halves(mm(value, pick[GROUP_COL:COLS, :]))
+
+    for copy in edge_round:
+        copy.wait()
+    value = jnp.concatenate([recv_e2[0], recv_e2[1]], axis=1)
+    value = two_terms(by_level(slot_level[:, 0:256], backward, value))
+    total = faces[...] + halves(mm(value, pick[M_DEV:GROUP_COL, :]))
     add_rows(pl.ds(0, 64, stride=8), total[:, 1024:1280])
     add_rows(pl.ds(7, 64, stride=8), total[:, 1280:1536])
     for i in range(8):
@@ -482,10 +484,12 @@
             pltpu.VMEM((128, 128), F32),
             pltpu.VMEM((2, 64, 128), F32),
             pltpu.VMEM((128, 128), F32),
-            pltpu.VMEM((2, 80, 128), F32),
+            pltpu.VMEM((2, 64, 128), F32),
             pltpu.VMEM((64, 128), F32),
-            pltpu.VMEM((2, 80, 128), F32),
+            pltpu.VMEM((2, 64, 128), F32),
             pltpu.VMEM((64, 128), F32),
+            pltpu.VMEM((2, 16, 128), F32),
+            pltpu.VMEM((2, 16, 128), F32),
             dma((9,)),
             dma((2,)),
             dma((2,)),
@@ -495,6 +499,8 @@
             dma((2,)),
             dma((7,)),
             dma((7,)),
+            dma((2,)),
+            dma((2,)),
         ],
         compiler_params=pltpu.CompilerParams(
             collective_id=0, has_side_effects=True, vmem_limit_bytes=48 * 1024 * 1024

time: 29.3 us -> 28.9 us (0.986)
  Pallas kernels: 28.3 us -> 28 us
where the time goes in v4:
time: 28.9 us; the launch traced here: 28.8 us
  Pallas kernels  28 us (97%)
  local copies, waits for them, and re-layouts  0.8 us (3%)
    pallas_call x1, Pallas kernels, on_device(): pl.pallas_call(functools.partial(kernel, n_elem), out_shape=jax.ShapeDtyp...  28 us
    unnamed x1, local copies, waits for them, and re-layouts  0.8 us

profile of v4, /device:TPU:1, one launch (start us, length us, event | category | flops | bytes accessed | tf_op | source)
XLA Modules:
  0.0 28.8 jit_solution(13194212604191041231)
XLA Ops:
  0.0 28.0 %shard_map.82 = f32[512,256]{1,0:T(8,128)S(1)} custom-call(f32[512,256]{1,0:T(8,128)} %u_hbm.1, bf16[3,512,256]{2,1,0:T(8,128)(2,1)} %met_hbm.1, f32[8,8]{1,0:T(8,128)} %deriv_hbm.1, f32[2,8,8]{2,1,0:T(8,128)} %interp_hbm.1, s32[12,128]{1,0:T(8,128)} %bitcast.3, s32[12,128]{1,0:T(8,128)} %bitcast.4, s32[3,128]{1,0:T(4,128)} %bitcast.5, s32[8,256]{1,0:T(8,128)} %vid_hbm.1), custom_call_target="tpu_custom_call" | custom-call | tf_op jit(solution)/shard_map/pallas_call | solution.py:455
  28.0 0.8 %copy.10 = f32[512,256]{1,0:T(8,128)} copy(f32[512,256]{1,0:T(8,128)S(1)} %shard_map.82) | data formatting | bytes 1048576

commit v5 on v4

--- a/solution.py
+++ b/solution.py
@@ -84,11 +84,13 @@
     pick,
     pick2,
     corner_hot,
-    proj,
+    terms,
+    slot_level,
     own,
     faces,
     answers,
     arrived,
+    returned,
     same,
     grad0,
     acc,
@@ -219,20 +221,21 @@
         return chosen
 
     far = [slice(8 * j, 8 * j + 8) for j in range(64)]
-    trace = jnp.concatenate(
-        [
-            node_rows(u, slice(0, 64)),
-            node_rows(u, slice(448, 512)),
-            jnp.concatenate([node_rows(u, far[8 * i]) for i in range(8)], axis=0),
-            jnp.concatenate([node_rows(u, far[8 * i + 7]) for i in range(8)], axis=0),
-            node_rows(u, pl.ds(0, 64, stride=8)),
-            node_rows(u, pl.ds(7, 64, stride=8)),
-        ],
-        axis=1,
-    )
-    hi, lo = split(by_level(across(lvl, 0, 12), forth, trace))
-    proj[0:64, :] = hi
-    proj[64:128, :] = lo
+    def traces():
+        return jnp.concatenate(
+            [
+                node_rows(u, slice(0, 64)),
+                node_rows(u, slice(448, 512)),
+                jnp.concatenate([node_rows(u, far[8 * i]) for i in range(8)], axis=0),
+                jnp.concatenate([node_rows(u, far[8 * i + 7]) for i in range(8)], axis=0),
+                node_rows(u, pl.ds(0, 64, stride=8)),
+                node_rows(u, pl.ds(7, 64, stride=8)),
+            ],
+            axis=1,
+        )
+
+    terms[0:128, :] = two_terms(traces())
+    terms[128:144, :] = across(lvl, 0, 12)[0:16].astype(F32).astype(BF16)
 
     away = vid[...] - e * NV_DEV
     total_vertices = n_elem * NV_DEV
@@ -258,7 +261,9 @@
         sums = sums + mm(jnp.concatenate(parts, axis=0).astype(BF16), hot, NT)
     local = jnp.concatenate([sums[0:8] + sums[8:16], sums[16:24]], axis=0)
 
-    leaving = halves(mm(proj[...], pick[M_DEV:COLS, :], NT))
+    raw = mm(terms[...], pick[M_DEV:COLS, :], NT)
+    slot_level[...] = jnp.broadcast_to(raw[128:129], (64, SLOTS))
+    leaving = by_level(slot_level[...], forth, halves(raw[0:128]))
     send_e[0] = leaving[:, 0:128]
     send_e[1] = leaving[:, 128:256]
     turned = jnp.concatenate([leaving[:, 256:384], jnp.zeros((64, 128), F32)], axis=0).T
@@ -302,7 +307,9 @@
     recv_g[mine, :] = send_g[mine, :]
 
     fill_pick(0, M_DEV)
-    own[...] = halves(mm(proj[...], pick[0:M_DEV, :], NT))
+    own[...] = halves(
+        mm(two_terms(by_level(across(lvl, 0, 12), forth, traces())), pick[0:M_DEV, :], NT)
+    )
     loads[7].wait()
     rows2 = iota((M_DEV, 128), 0)
     for b in range(SLOTS // 128):
@@ -315,11 +322,6 @@
         ma[24 + 8 * which : 32 + 8 * which, :] = wide[:, 0:192]
         mb[24 + 8 * which : 32 + 8 * which, :] = wide[:, 192:384]
     backward = three_terms(jnp.concatenate([kron(r + 3, s + 3) for r, s in pairs], axis=0))
-
-    level_row = jnp.concatenate([lvl[n : n + 1, :] for n in range(12)], axis=1)
-    level_row = jnp.broadcast_to(level_row, (16, FACES)).astype(F32).astype(BF16)
-    slot_level = mm(level_row, pick[M_DEV:COLS, :], NT)[0:1]
-    slot_level = jnp.broadcast_to(slot_level, (64, SLOTS))
 
     slot_row = jnp.concatenate([slot[b : b + 1, :] for b in range(3)], axis=1)
     for b in range(3):
@@ -339,14 +341,11 @@
     coarse_round = edge_copies(send_c, recv_c, sc_sem, rc_sem)
     for copy in coarse_round:
         copy.start()
-    from_group = two_terms(group_in.T[0:64])
-    arrived[:, 256:384] = from_group
-    answers[...] = answers[...] + halves(mm(from_group, same[256:384, :]))
+    arrived[:, 256:384] = two_terms(group_in.T[0:64])
     for copy in edge_round:
         copy.wait()
-    from_edge = two_terms(jnp.concatenate([recv_e[0], recv_e[1]], axis=1))
-    arrived[:, 0:256] = from_edge
-    answer = answers[...] + halves(mm(from_edge, same[0:256, :]))
+    arrived[:, 0:256] = two_terms(jnp.concatenate([recv_e[0], recv_e[1]], axis=1))
+    answer = answers[...] + halves(mm(arrived[...], same[...]))
     send_e2[0] = answer[:, 0:128]
     send_e2[1] = answer[:, 128:256]
     edge_round = edge_copies(send_e2, recv_e2, se2_sem, re2_sem)
@@ -428,14 +427,13 @@
     ).T
     odd = (iota((64, 128), 1) & 8) != 0
     value = jnp.where(odd, turned[64:128], turned[0:64])
-    value = two_terms(by_level(slot_level[:, 256:384], backward, value))
-    faces[...] = faces[...] + halves(mm(value, pick[GROUP_COL:COLS, :]))
+    returned[:, 256:384] = two_terms(by_level(slot_level[:, 256:384], backward, value))
 
     for copy in edge_round:
         copy.wait()
     value = jnp.concatenate([recv_e2[0], recv_e2[1]], axis=1)
-    value = two_terms(by_level(slot_level[:, 0:256], backward, value))
-    total = faces[...] + halves(mm(value, pick[M_DEV:GROUP_COL, :]))
+    returned[:, 0:256] = two_terms(by_level(slot_level[:, 0:256], backward, value))
+    total = faces[...] + halves(mm(returned[...], pick[M_DEV:COLS, :]))
     add_rows(pl.ds(0, 64, stride=8), total[:, 1024:1280])
     add_rows(pl.ds(7, 64, stride=8), total[:, 1280:1536])
     for i in range(8):
@@ -472,10 +470,12 @@
             pltpu.VMEM((COLS, FACES), BF16),
             pltpu.VMEM((M_DEV, SLOTS), BF16),
             pltpu.VMEM((128, 8 * E_DEV), BF16),
-            pltpu.VMEM((128, FACES), BF16),
+            pltpu.VMEM((144, FACES), BF16),
+            pltpu.VMEM((64, SLOTS), F32),
             pltpu.VMEM((64, M_DEV), F32),
             pltpu.VMEM((64, FACES), F32),
             pltpu.VMEM((64, SLOTS), F32),
+            pltpu.VMEM((128, SLOTS), BF16),
             pltpu.VMEM((128, SLOTS), BF16),
             pltpu.VMEM((SLOTS, SLOTS), BF16),
             pltpu.VMEM((NODES, E_DEV), F32),

time: 28.9 us -> 28.7 us (level)
  Pallas kernels: 28 us -> 27.7 us
where the time goes in v5:
time: 28.7 us; the launch traced here: 28.5 us
  Pallas kernels  27.7 us (97%)
  local copies, waits for them, and re-layouts  0.8 us (3%)
    pallas_call x1, Pallas kernels, on_device(): pl.pallas_call(functools.partial(kernel, n_elem), out_shape=jax.ShapeDtyp...  27.7 us
    unnamed x1, local copies, waits for them, and re-layouts  0.8 us

profile of v5, /device:TPU:1, one launch (start us, length us, event | category | flops | bytes accessed | tf_op | source)
XLA Modules:
  0.0 28.5 jit_solution(6679472393429877183)
XLA Ops:
  0.0 27.7 %shard_map.82 = f32[512,256]{1,0:T(8,128)S(1)} custom-call(f32[512,256]{1,0:T(8,128)} %u_hbm.1, bf16[3,512,256]{2,1,0:T(8,128)(2,1)} %met_hbm.1, f32[8,8]{1,0:T(8,128)} %deriv_hbm.1, f32[2,8,8]{2,1,0:T(8,128)} %interp_hbm.1, s32[12,128]{1,0:T(8,128)} %bitcast.3, s32[12,128]{1,0:T(8,128)} %bitcast.4, s32[3,128]{1,0:T(4,128)} %bitcast.5, s32[8,256]{1,0:T(8,128)} %vid_hbm.1), custom_call_target="tpu_custom_call" | custom-call | tf_op jit(solution)/shard_map/pallas_call | solution.py:453
  27.7 0.8 %copy.10 = f32[512,256]{1,0:T(8,128)} copy(f32[512,256]{1,0:T(8,128)S(1)} %shard_map.82) | data formatting | bytes 1048576

commit v6 on v5

--- a/solution.py
+++ b/solution.py
@@ -13,7 +13,6 @@
 M_DEV = 512
 SLOTS = 2 * CAP_E + GROUP * CAP_C
 COLS = M_DEV + SLOTS
-GROUP_COL = M_DEV + 2 * CAP_E
 NV_DEV = 256
 E_DEV = 256
 FACES = 6 * E_DEV
@@ -69,7 +68,10 @@
     tgt_hbm,
     slot_hbm,
     vid_hbm,
-    out,
+    acc,
+    faces,
+    returned,
+    sent,
     u,
     met,
     deriv,
@@ -87,13 +89,10 @@
     terms,
     slot_level,
     own,
-    faces,
     answers,
     arrived,
-    returned,
     same,
     grad0,
-    acc,
     send_e,
     send_g,
     recv_e,
@@ -154,17 +153,20 @@
         for side in range(2):
             acc[side, place, :] = acc[side, place, :] + value[:, 128 * side : 128 * side + 128]
 
-    def fill_pick(first, last):
+    def fill_pick(ref, first, last):
         rows = iota((last - first, 128), 0) + first
-        for b in range(FACES // 128):
-            hot = jnp.where(rows == tgt[b : b + 1, :], 1.0, 0.0).astype(BF16)
-            pick[first:last, b * 128 : (b + 1) * 128] = hot
+        for side in range(2):
+            for f in range(6):
+                row = 2 * f + side
+                place = 128 * (6 * side + f)
+                hot = jnp.where(rows == tgt[row : row + 1, :], 1.0, 0.0).astype(BF16)
+                ref[:, place : place + 128] = hot
 
     small[...] = jnp.zeros_like(small)
     for load in loads[:7]:
         load.wait()
     loads[8].start()
-    fill_pick(M_DEV, COLS)
+    fill_pick(sent, M_DEV, COLS)
 
     small[0:8, 0:8] = interp[0]
     small[8:16, 0:8] = interp[1]
@@ -209,9 +211,10 @@
     pairs = [(0, 0), (0, 1), (1, 0), (1, 1)]
     forth = three_terms(jnp.concatenate([kron(r, s) for r, s in pairs], axis=0))
 
-    def across(ref, first, count):
-        row = jnp.concatenate([ref[n : n + 1, :] for n in range(first, first + count)], axis=1)
-        return jnp.broadcast_to(row, (64, 128 * count))
+    def across(rows):
+        order = [2 * f + side for side in range(2) for f in range(6)]
+        row = jnp.concatenate([lvl[n : n + 1, :] for n in order], axis=1)
+        return jnp.broadcast_to(row, (rows, FACES))
 
     def by_level(level, mats, value):
         every = mm(mats, stacked(value))
@@ -222,20 +225,20 @@
 
     far = [slice(8 * j, 8 * j + 8) for j in range(64)]
     def traces():
-        return jnp.concatenate(
-            [
-                node_rows(u, slice(0, 64)),
-                node_rows(u, slice(448, 512)),
-                jnp.concatenate([node_rows(u, far[8 * i]) for i in range(8)], axis=0),
-                jnp.concatenate([node_rows(u, far[8 * i + 7]) for i in range(8)], axis=0),
-                node_rows(u, pl.ds(0, 64, stride=8)),
-                node_rows(u, pl.ds(7, 64, stride=8)),
-            ],
-            axis=1,
-        )
+        parts = []
+        for side in range(2):
+            parts += [
+                u[side, 0:64, :],
+                u[side, 448:512, :],
+                jnp.concatenate([u[side, far[8 * i], :] for i in range(8)], axis=0),
+                jnp.concatenate([u[side, far[8 * i + 7], :] for i in range(8)], axis=0),
+                u[side, pl.ds(0, 64, stride=8), :],
+                u[side, pl.ds(7, 64, stride=8), :],
+            ]
+        return jnp.concatenate(parts, axis=1)
 
     terms[0:128, :] = two_terms(traces())
-    terms[128:144, :] = across(lvl, 0, 12)[0:16].astype(F32).astype(BF16)
+    terms[128:144, :] = across(16).astype(F32).astype(BF16)
 
     away = vid[...] - e * NV_DEV
     total_vertices = n_elem * NV_DEV
@@ -261,7 +264,7 @@
         sums = sums + mm(jnp.concatenate(parts, axis=0).astype(BF16), hot, NT)
     local = jnp.concatenate([sums[0:8] + sums[8:16], sums[16:24]], axis=0)
 
-    raw = mm(terms[...], pick[M_DEV:COLS, :], NT)
+    raw = mm(terms[...], sent[...], NT)
     slot_level[...] = jnp.broadcast_to(raw[128:129], (64, SLOTS))
     leaving = by_level(slot_level[...], forth, halves(raw[0:128]))
     send_e[0] = leaving[:, 0:128]
@@ -306,9 +309,9 @@
     mine = pl.ds(pl.multiple_of(c * CAP_C, CAP_C), CAP_C)
     recv_g[mine, :] = send_g[mine, :]
 
-    fill_pick(0, M_DEV)
+    fill_pick(pick, 0, M_DEV)
     own[...] = halves(
-        mm(two_terms(by_level(across(lvl, 0, 12), forth, traces())), pick[0:M_DEV, :], NT)
+        mm(two_terms(by_level(across(64), forth, traces())), pick[...], NT)
     )
     loads[7].wait()
     rows2 = iota((M_DEV, 128), 0)
@@ -393,8 +396,8 @@
             add_rows(slice(64 * i + 8 * j, 64 * i + 8 * j + 8), back[8 * i : 8 * i + 8])
 
     mortar = own[...] + halves(mm(arrived[...], pick2[...], NT))
-    picked = halves(mm(two_terms(mortar), pick[0:M_DEV, :]))
-    faces[...] = by_level(across(lvl, 0, 12), backward, picked)
+    picked = halves(mm(two_terms(mortar), pick[...]))
+    faces[...] = by_level(across(64), backward, picked)
 
     for copy in coarse_round:
         copy.wait()
@@ -433,28 +436,48 @@
         copy.wait()
     value = jnp.concatenate([recv_e2[0], recv_e2[1]], axis=1)
     returned[:, 0:256] = two_terms(by_level(slot_level[:, 0:256], backward, value))
-    total = faces[...] + halves(mm(returned[...], pick[M_DEV:COLS, :]))
-    add_rows(pl.ds(0, 64, stride=8), total[:, 1024:1280])
-    add_rows(pl.ds(7, 64, stride=8), total[:, 1280:1536])
-    for i in range(8):
-        block = node_rows(acc, slice(64 * i, 64 * i + 64))
-        if i == 0:
-            block = block + total[:, 0:256]
-        if i == 7:
-            block = block + total[:, 256:512]
-        near = block[0:8] + total[8 * i : 8 * i + 8, 512:768]
-        away = block[56:64] + total[8 * i : 8 * i + 8, 768:1024]
-        out[64 * i : 64 * i + 64, :] = jnp.concatenate([near, block[8:56], away], axis=0)
+
+
+def write(acc, faces, returned, sent, out, buf, sem):
+    copies = []
+    for side in range(2):
+        span = slice(768 * side, 768 * side + 768)
+        total = faces[:, span] + halves(mm(returned[...], sent[:, span]))
+        for i in range(8):
+            rows = slice(64 * i, 64 * i + 64)
+            block = acc[side, rows, :]
+            if i == 0:
+                block = block + total[:, 0:128]
+            if i == 7:
+                block = block + total[:, 128:256]
+            near = block[0:8] + total[8 * i : 8 * i + 8, 256:384]
+            away = block[56:64] + total[8 * i : 8 * i + 8, 384:512]
+            buf[side, rows, :] = jnp.concatenate([near, block[8:56], away], axis=0)
+        for first, part in ((0, total[:, 512:640]), (7, total[:, 640:768])):
+            rows = pl.ds(first, 64, stride=8)
+            buf[side, rows, :] = buf[side, rows, :] + part
+        copy = pltpu.make_async_copy(
+            buf.at[side], out.at[:, 128 * side : 128 * side + 128], sem.at[side]
+        )
+        copy.start()
+        copies.append(copy)
+    for copy in copies:
+        copy.wait()
 
 
 def on_device(n_elem, nodal, metric, derivative, interp, face_level, face_target, slot_mortar, vertex_ids):
     anywhere = pl.BlockSpec(memory_space=pltpu.HBM)
     dma = pltpu.SemaphoreType.DMA
-    return pl.pallas_call(
+    parts = pl.pallas_call(
         functools.partial(kernel, n_elem),
-        out_shape=jax.ShapeDtypeStruct((NODES, E_DEV), F32),
+        out_shape=[
+            jax.ShapeDtypeStruct((2, NODES, 128), F32),
+            jax.ShapeDtypeStruct((64, FACES), F32),
+            jax.ShapeDtypeStruct((128, SLOTS), BF16),
+            jax.ShapeDtypeStruct((SLOTS, FACES), BF16),
+        ],
         in_specs=[anywhere] * 8,
-        out_specs=pl.BlockSpec(memory_space=pltpu.VMEM),
+        out_specs=[pl.BlockSpec(memory_space=pltpu.VMEM)] * 4,
         scratch_shapes=[
             pltpu.VMEM((2, NODES, 128), F32),
             pltpu.VMEM((3, NODES, E_DEV), BF16),
@@ -467,19 +490,16 @@
             pltpu.VMEM((12, 128), jnp.int32),
             pltpu.VMEM((3, 128), jnp.int32),
             pltpu.VMEM((8, E_DEV), jnp.int32),
-            pltpu.VMEM((COLS, FACES), BF16),
+            pltpu.VMEM((M_DEV, FACES), BF16),
             pltpu.VMEM((M_DEV, SLOTS), BF16),
             pltpu.VMEM((128, 8 * E_DEV), BF16),
             pltpu.VMEM((144, FACES), BF16),
             pltpu.VMEM((64, SLOTS), F32),
             pltpu.VMEM((64, M_DEV), F32),
-            pltpu.VMEM((64, FACES), F32),
             pltpu.VMEM((64, SLOTS), F32),
-            pltpu.VMEM((128, SLOTS), BF16),
             pltpu.VMEM((128, SLOTS), BF16),
             pltpu.VMEM((SLOTS, SLOTS), BF16),
             pltpu.VMEM((NODES, E_DEV), F32),
-            pltpu.VMEM((2, NODES, 128), F32),
             pltpu.VMEM((2, 64, 128), F32),
             pltpu.VMEM((128, 128), F32),
             pltpu.VMEM((2, 64, 128), F32),
@@ -520,6 +540,13 @@
             )
         ]
     )
+    return pl.pallas_call(
+        write,
+        out_shape=jax.ShapeDtypeStruct((NODES, E_DEV), F32),
+        in_specs=[pl.BlockSpec(memory_space=pltpu.VMEM)] * 4,
+        out_specs=pl.BlockSpec(memory_space=pltpu.HBM),
+        scratch_shapes=[pltpu.VMEM((2, NODES, 128), F32), dma((2,))],
+    )(*[pltpu.with_memory_space_constraint(part, pltpu.VMEM) for part in parts])
 
 
 def solution(mesh):

time: 28.7 us -> 28.6 us (level)
  local copies, waits for them, and re-layouts: 0.8 us -> 0 us
  Pallas kernels: 27.7 us -> 28.4 us
    unnamed x1 -> x0, local copies, waits for them, and re-layouts: 0.8 us -> none
    pallas_call x1 -> x2, Pallas kernels: 27.7 us -> 28.4 us  [the longest x1 27.3 us: on_device(): pl.pallas_call(functools.partial(kernel, n_elem), out_shape=[jax.ShapeDty...]
where the time goes in v6:
time: 28.6 us; the launch traced here: 28.5 us
  Pallas kernels  28.4 us (99%)
    pallas_call x1, Pallas kernels, on_device(): pl.pallas_call(functools.partial(kernel, n_elem), out_shape=[jax.ShapeDty...  27.3 us
    pallas_call x1, Pallas kernels, on_device(): pl.pallas_call(write, out_shape=jax.ShapeDtypeStruct((NODES, E_DEV), F32)...  1.12 us

profile of v6, /device:TPU:1, one launch (start us, length us, event | category | flops | bytes accessed | tf_op | source)
XLA Modules:
  0.0 28.5 jit_solution(6469115085887584298)
XLA Ops:
  0.0 27.3 %shard_map.82 = (f32[2,512,128]{2,1,0:T(8,128)S(1)}, f32[64,1536]{1,0:T(8,128)S(1)}, bf16[128,384]{1,0:T(8,128)(2,1)S(1)}, bf16[384,1536]{1,0:T(8,128)(2,1)S(1)}) custom-call(f32[512,256]{1,0:T(8,128)} %u_hbm.1, bf16[3,512,256]{2,1,0:T(8,128)(2,1)} %met_hbm.1, f32[8,8]{1,0:T(8,128)} %deriv_hbm.1, f32[2,8,8]{2,1,0:T(8,128)} %interp_hbm.1, s32[12,128]{1,0:T(8,128)} %bitcast.3, ...), custom_call_target="tpu_custom_call" | custom-call | tf_op jit(solution)/shard_map/pallas_call | solution.py:471
  27.3 1.1 %shard_map.83 = f32[512,256]{1,0:T(8,128)} custom-call(f32[2,512,128]{2,1,0:T(8,128)S(1)} %get-tuple-element.9.acc, f32[64,1536]{1,0:T(8,128)S(1)} %get-tuple-element.10.faces, bf16[128,384]{1,0:T(8,128)(2,1)S(1)} %get-tuple-element.11.returned, bf16[384,1536]{1,0:T(8,128)(2,1)S(1)} %get-tuple-element.12.sent), custom_call_target="tpu_custom_call" | custom-call | tf_op jit(solution)/shard_map/pallas_call | solution.py:543

commit v7 on v6

--- a/solution.py
+++ b/solution.py
@@ -443,24 +443,29 @@
     for side in range(2):
         span = slice(768 * side, 768 * side + 768)
         total = faces[:, span] + halves(mm(returned[...], sent[:, span]))
-        for i in range(8):
-            rows = slice(64 * i, 64 * i + 64)
-            block = acc[side, rows, :]
-            if i == 0:
-                block = block + total[:, 0:128]
-            if i == 7:
-                block = block + total[:, 128:256]
-            near = block[0:8] + total[8 * i : 8 * i + 8, 256:384]
-            away = block[56:64] + total[8 * i : 8 * i + 8, 384:512]
-            buf[side, rows, :] = jnp.concatenate([near, block[8:56], away], axis=0)
-        for first, part in ((0, total[:, 512:640]), (7, total[:, 640:768])):
-            rows = pl.ds(first, 64, stride=8)
-            buf[side, rows, :] = buf[side, rows, :] + part
-        copy = pltpu.make_async_copy(
-            buf.at[side], out.at[:, 128 * side : 128 * side + 128], sem.at[side]
-        )
-        copy.start()
-        copies.append(copy)
+        for quarter in range(2):
+            for i in range(4 * quarter, 4 * quarter + 4):
+                rows = slice(64 * i, 64 * i + 64)
+                block = acc[side, rows, :]
+                if i == 0:
+                    block = block + total[:, 0:128]
+                if i == 7:
+                    block = block + total[:, 128:256]
+                near = block[0:8] + total[8 * i : 8 * i + 8, 256:384]
+                away = block[56:64] + total[8 * i : 8 * i + 8, 384:512]
+                buf[side, rows, :] = jnp.concatenate([near, block[8:56], away], axis=0)
+            half = slice(32 * quarter, 32 * quarter + 32)
+            for first, part in ((0, total[half, 512:640]), (7, total[half, 640:768])):
+                rows = pl.ds(256 * quarter + first, 32, stride=8)
+                buf[side, rows, :] = buf[side, rows, :] + part
+            rows = slice(256 * quarter, 256 * quarter + 256)
+            copy = pltpu.make_async_copy(
+                buf.at[side, rows],
+                out.at[rows, 128 * side : 128 * side + 128],
+                sem.at[2 * side + quarter],
+            )
+            copy.start()
+            copies.append(copy)
     for copy in copies:
         copy.wait()
 
@@ -545,7 +550,7 @@
         out_shape=jax.ShapeDtypeStruct((NODES, E_DEV), F32),
         in_specs=[pl.BlockSpec(memory_space=pltpu.VMEM)] * 4,
         out_specs=pl.BlockSpec(memory_space=pltpu.HBM),
-        scratch_shapes=[pltpu.VMEM((2, NODES, 128), F32), dma((2,))],
+        scratch_shapes=[pltpu.VMEM((2, NODES, 128), F32), dma((4,))],
     )(*[pltpu.with_memory_space_constraint(part, pltpu.VMEM) for part in parts])
 
 

time: 28.6 us -> 28.6 us (level)
  no operation moved by 1% of the time
where the time goes in v7:
time: 28.6 us; the launch traced here: 28.5 us
  Pallas kernels  28.4 us (99%)
    pallas_call x1, Pallas kernels, on_device(): pl.pallas_call(functools.partial(kernel, n_elem), out_shape=[jax.ShapeDty...  27.3 us
    pallas_call x1, Pallas kernels, on_device(): pl.pallas_call(write, out_shape=jax.ShapeDtypeStruct((NODES, E_DEV), F32)...  1.12 us

profile of v7, /device:TPU:1, one launch (start us, length us, event | category | flops | bytes accessed | tf_op | source)
XLA Modules:
  0.0 28.5 jit_solution(16579332645919998262)
XLA Ops:
  0.0 27.3 %shard_map.82 = (f32[2,512,128]{2,1,0:T(8,128)S(1)}, f32[64,1536]{1,0:T(8,128)S(1)}, bf16[128,384]{1,0:T(8,128)(2,1)S(1)}, bf16[384,1536]{1,0:T(8,128)(2,1)S(1)}) custom-call(f32[512,256]{1,0:T(8,128)} %u_hbm.1, bf16[3,512,256]{2,1,0:T(8,128)(2,1)} %met_hbm.1, f32[8,8]{1,0:T(8,128)} %deriv_hbm.1, f32[2,8,8]{2,1,0:T(8,128)} %interp_hbm.1, s32[12,128]{1,0:T(8,128)} %bitcast.3, ...), custom_call_target="tpu_custom_call" | custom-call | tf_op jit(solution)/shard_map/pallas_call | solution.py:476
  27.3 1.1 %shard_map.83 = f32[512,256]{1,0:T(8,128)} custom-call(f32[2,512,128]{2,1,0:T(8,128)S(1)} %get-tuple-element.9.acc, f32[64,1536]{1,0:T(8,128)S(1)} %get-tuple-element.10.faces, bf16[128,384]{1,0:T(8,128)(2,1)S(1)} %get-tuple-element.11.returned, bf16[384,1536]{1,0:T(8,128)(2,1)S(1)} %get-tuple-element.12.sent), custom_call_target="tpu_custom_call" | custom-call | tf_op jit(solution)/shard_map/pallas_call | solution.py:548
